TPU v7x, 128 devices: a whole 4x4x4 slice. The times are simulated.
128 devices in a mesh: row: 8 (over y, core), col: 16 (over x, z).
Axes of the slice: x: 4, y: 4, z: 4, core: 2. Of those that a mesh axis runs over, the one named last changes fastest.
Arguments:
- object_amp: float32 [4, 4096, 8192], P(None, 'row', 'col'), may hold values from 0.5 to 1.5
- object_phase: float32 [4, 4096, 8192], P(None, 'row', 'col'), may hold values from -3.140625 to 3.140625
- probe_field: float32 [2, 256, 256], replicated, may hold values from -5 to 5
- measured: float32 [8, 16, 4, 256, 256], P('row', 'col'), may hold values from 0 to 2
- offsets: int32 [8, 16, 4, 2], P('row', 'col'), may hold values from 0 to 512
- counts: int32 [8, 16], P('row', 'col'), may hold values from 1 to 4, as said below
Outputs:
- new_real: float32 [4, 4096, 8192], P(None, 'row', 'col')
- new_imag: float32 [4, 4096, 8192], P(None, 'row', 'col')
Inputs may be any that keep to these rules, and one draw needn't show every extreme that they name: `counts`: every count is at least one, and some tile uses all 4 slots. Slots at or beyond a tile's count are unused. `offsets`: entries of unused slots carry no meaning.
All inputs are finite; a program needn't handle non-finite values.
Results may differ from a plain program's by a relative error of at most 0.0003.
Values sent between devices are 32-bit elements; how exact they have to be, the bound alone decides.
No kernel may reach another device: no remote copies, remote signals or barrier semaphores. Data moves between devices by JAX's collectives and lax.ppermute only.
A program may use at most 192 MiB of HBM per device.

v0:
```python
import jax
import jax.numpy as jnp
import numpy as np
from jax import lax
from jax.experimental import pallas as pl
from jax.experimental.pallas import tpu as pltpu
from jax.sharding import PartitionSpec as P


FRESNEL = 0.0005
N = 256
H = 128
SLICES = 4
SLOTS = 4
TILE = 512
F32 = jnp.float32
BF16 = jnp.bfloat16

SEGMENTS = ((0, H, 0, H), (1, 0, H, N), (2, 0, H + N, H))


def real_form(matrix):
    return np.block([[matrix.real, -matrix.imag], [matrix.imag, matrix.real]])


def split_table(pair):
    parts = np.stack([real_form(m) for m in pair]).astype(np.float32)
    high = parts.astype(BF16)
    low = (parts - high.astype(np.float32)).astype(BF16)
    return np.stack([high, low])


def tables():
    counter = np.arange(N)
    frequency = (counter + H) % N - H
    q = np.exp(1j * FRESNEL * frequency.astype(np.float64) ** 2)
    spread = np.fft.ifft(q)
    j, m = np.arange(H)[:, None], np.arange(H)[None, :]
    near, far = spread[(j - m) % N], spread[(j - m - H) % N]
    prop = ((near + far) / 2, (near - far) / 2)
    even = np.exp(-2j * np.pi * ((j * m) % H) / H) / 16
    odd = np.exp(-2j * np.pi * ((m * (2 * j + 1)) % N) / N) / 16
    prop_table, dft_table = split_table(prop), split_table((even, odd))
    return prop_table, dft_table


def fit_sincos():
    u = np.cos(np.linspace(0, np.pi, 4001)) * 0.79
    w = u * u
    sin_part = np.polynomial.polynomial.polyfit(w, np.where(u == 0, 1.0, np.sin(u) / np.where(u == 0, 1.0, u)), 4)
    cos_part = np.polynomial.polynomial.polyfit(w, np.cos(u), 4)
    return [float(c) for c in sin_part], [float(c) for c in cos_part]


SIN_PART, COS_PART = fit_sincos()


def poly(w, coefficients):
    total = jnp.full_like(w, coefficients[-1])
    for c in coefficients[-2::-1]:
        total = total * w + c
    return total


def sincos(phase):
    u = phase * 0.25
    w = u * u
    s, c = u * poly(w, SIN_PART), poly(w, COS_PART)
    s, c = 2.0 * s * c, 1.0 - 2.0 * s * s
    return 2.0 * s * c, 1.0 - 2.0 * s * s


def split(x):
    high = x.astype(BF16)
    return high, (x - high.astype(F32)).astype(BF16)


def dot(a, b):
    return jnp.dot(a, b, preferred_element_type=F32)


def left_product(table, which, z):
    zh, zl = split(z)
    mh, ml = table[0, which], table[1, which]
    return dot(mh, zh) + dot(ml, zh) + dot(mh, zl)


def right_product(table, which, z):
    zh, zl = split(z)
    mh, ml = table[0, which], table[1, which]
    return dot(zh, mh) + dot(zh, ml) + dot(zl, mh)


def halves(x, axis):
    return (x[:H], x[H:]) if axis == 0 else (x[:, :H], x[:, H:])


def along(wave, axis, table, before, after):
    (r0, r1), (i0, i1) = halves(wave[0], axis), halves(wave[1], axis)
    if before:
        r0, r1, i0, i1 = r0 + r1, r0 - r1, i0 + i1, i0 - i1
    product = left_product if axis == 0 else right_product
    first = product(table, 0, jnp.concatenate([r0, i0], axis))
    second = product(table, 1, jnp.concatenate([r1, i1], axis))
    (r0, i0), (r1, i1) = halves(first, axis), halves(second, axis)
    if after:
        r0, r1, i0, i1 = r0 + r1, r0 - r1, i0 + i1, i0 - i1
    return jnp.concatenate([r0, r1], axis), jnp.concatenate([i0, i1], axis)


def both_axes(wave, left, right, before, after):
    wave = along(wave, 0, left, before, after)
    return along(wave, 1, right, before, after)


def product_of(a, b):
    return a[0] * b[0] - a[1] * b[1], a[0] * b[1] + a[1] * b[0]


def conj_product(a, b):
    return a[0] * b[0] + a[1] * b[1], a[0] * b[1] - a[1] * b[0]


class Place:
    def __init__(self, offs, j):
        top, left = offs[0, 0, j, 0], offs[0, 0, j, 1]
        self.t0, self.l0 = lax.shift_right_logical(top, 8), lax.shift_right_logical(left, 8)
        self.tr, self.lr = top & (N - 1), left & (N - 1)
        self.t1, self.l1 = jnp.minimum(self.t0 + 1, 2), jnp.minimum(self.l0 + 1, 2)
        self.rows = lax.broadcasted_iota(jnp.int32, (N, N), 0) >= self.tr
        self.cols = lax.broadcasted_iota(jnp.int32, (N, N), 1) >= self.lr

    def take(self, blocks, plane):
        upper = jnp.where(self.cols, blocks[plane, self.t0, self.l0], blocks[plane, self.t0, self.l1])
        lower = jnp.where(self.cols, blocks[plane, self.t1, self.l0], blocks[plane, self.t1, self.l1])
        return jnp.where(self.rows, upper, lower)

    def add(self, blocks, plane, value):
        upper = jnp.where(self.rows, value, 0.0)
        lower = jnp.where(self.rows, 0.0, value)
        for t, part in ((self.t0, upper), (self.t1, lower)):
            blocks[plane, t, self.l0] += jnp.where(self.cols, part, 0.0)
            blocks[plane, t, self.l1] += jnp.where(self.cols, 0.0, part)

    def shifted(self, probe):
        return tuple(pltpu.roll(pltpu.roll(probe[p], self.tr, 0), self.lr, 1) for p in range(2))


N_IN = 34


def fill_pairs(padded, s, k, amp, ph, left, right, above, below, corner_a, corner_b):
    pairs = []
    for rb, ro, rs, rn in SEGMENTS:
        rd, rr = pl.ds(ro, rn), pl.ds(rs, rn)
        for cb, co, cs, cn in SEGMENTS:
            for p, source in enumerate((amp, ph)):
                pairs.append((source.at[s, rr, pl.ds(cs, cn)], padded.at[p, rb, cb, rd, pl.ds(co, cn)]))
        pairs.append((left.at[:, k, rr, :], padded.at[:, rb, 0, rd, pl.ds(0, H)]))
        pairs.append((right.at[:, k, rr, :], padded.at[:, rb, 2, rd, pl.ds(H, H)]))
        pairs.append((above.at[:, s, :, rr], padded.at[:, 0, rb, pl.ds(0, H), rd]))
        pairs.append((below.at[:, s, :, rr], padded.at[:, 2, rb, pl.ds(H, H), rd]))
    for source, rb, ro in ((corner_a, 0, 0), (corner_b, 2, H)):
        pairs.append((source.at[:, k, :, pl.ds(0, H)], padded.at[:, rb, 0, pl.ds(ro, H), pl.ds(0, H)]))
        pairs.append((source.at[:, k, :, pl.ds(H, H)], padded.at[:, rb, 2, pl.ds(ro, H), pl.ds(H, H)]))
    return pairs


def copies_of(pairs, sems):
    return [pltpu.make_async_copy(a, b, sems.at[i]) for i, (a, b) in enumerate(pairs)]


def start_all(copies):
    for c in copies:
        c.start()


def wait_all(copies):
    for c in copies:
        c.wait()


def drain_pairs(totals, first, planes, by_columns, centre, top, bottom, left, right):
    own, pairs = pl.ds(first, planes), []
    for rb, ro, rs, rn in SEGMENTS:
        rd, rr = pl.ds(ro, rn), pl.ds(rs, rn)
        for cb, co, cs, cn in SEGMENTS:
            pairs.append((totals.at[own, rb, cb, rd, pl.ds(co, cn)], centre.at[:, rr, pl.ds(cs, cn)]))
        whole = pl.ds(rb * N, N)
        if by_columns:
            pairs.append((totals.at[own, rb, 0, :, pl.ds(0, H)], left.at[:, whole, :]))
            pairs.append((totals.at[own, rb, 2, :, pl.ds(H, H)], right.at[:, whole, :]))
            pairs.append((totals.at[own, 0, rb, pl.ds(0, H), rd], top.at[:, :, rr]))
            pairs.append((totals.at[own, 2, rb, pl.ds(H, H), rd], bottom.at[:, :, rr]))
        else:
            pairs.append((totals.at[own, rb, 0, rd, pl.ds(0, H)], left.at[:, rr, :]))
            pairs.append((totals.at[own, rb, 2, rd, pl.ds(H, H)], right.at[:, rr, :]))
            pairs.append((totals.at[own, 0, rb, pl.ds(0, H), :], top.at[:, :, whole]))
            pairs.append((totals.at[own, 2, rb, pl.ds(H, H), :], bottom.at[:, :, whole]))
    return pairs


def fold_shapes(planes, by_columns=False):
    shape = lambda *s: jax.ShapeDtypeStruct((planes, *s), F32)
    wide, tall = (TILE, 3 * N) if by_columns else (3 * N, TILE)
    return [shape(TILE, TILE), shape(H, wide), shape(H, wide), shape(tall, H), shape(tall, H)]


ANY = pl.BlockSpec(memory_space=pl.ANY)
SMEM = pl.BlockSpec(memory_space=pltpu.SMEM)
VMEM = pl.BlockSpec(memory_space=pltpu.VMEM)
PER_SLOT = pl.BlockSpec((1, 2, N, N), lambda j: (j, 0, 0, 0))
SLOT_SHAPE = jax.ShapeDtypeStruct((SLOTS, 2, N, N), F32)
PARAMS = pltpu.CompilerParams(dimension_semantics=("arbitrary",))
BLOCKS = lambda planes: pltpu.VMEM((planes, 3, 3, N, N), F32)


def window_of(padded, place):
    amp, ph = place.take(padded, 0), place.take(padded, 1)
    sine, cosine = sincos(ph)
    return amp * cosine, amp * sine


def intensity(wave):
    return wave[0] * wave[0] + wave[1] * wave[1]


def wave_in(ref):
    return ref[0, 0], ref[0, 1]


def put_wave(ref, wave):
    ref[0, 0], ref[0, 1] = wave


def enter(scalars, sides, probe, prop, prop_t):
    def kernel(offs, count, *rest):
        arrays, (probe, prop, prop_t) = rest[:8], rest[8:11]
        waves, window_ref, parts = rest[11:14], rest[14], rest[15:20]
        padded, totals, sems = rest[20:]
        j = pl.program_id(0)
        fills = [copies_of(fill_pairs(padded.at[s], s, s, *arrays), sems.at[s]) for s in range(2)]

        @pl.when(j == 0)
        def _():
            start_all(fills[0])
            start_all(fills[1])
            totals[...] = jnp.zeros_like(totals)
            wait_all(fills[0])

        @pl.when(j < count[0, 0])
        def _():
            place = Place(offs, j)
            wave = place.shifted(probe)
            put_wave(waves[0], wave)
            place.add(totals, 0, intensity(wave))
            wave = both_axes(product_of(wave, window_of(padded.at[0], place)), prop, prop_t, True, True)
            put_wave(waves[1], wave)
            place.add(totals, 1, intensity(wave))

        @pl.when(j == 0)
        def _():
            wait_all(fills[1])

        @pl.when(j < count[0, 0])
        def _():
            place = Place(offs, j)
            window = window_of(padded.at[1], place)
            put_wave(window_ref, window)
            wave = both_axes(product_of(wave_in(waves[1]), window), prop, prop_t, True, True)
            put_wave(waves[2], wave)
            place.add(totals, 2, intensity(wave))

        @pl.when(j == SLOTS - 1)
        def _():
            drains = copies_of(drain_pairs(totals, 0, 3, True, *parts), sems.at[0])
            start_all(drains)
            wait_all(drains)

    out = pl.pallas_call(
        kernel,
        name="enter",
        grid=(SLOTS,),
        in_specs=[SMEM, SMEM] + [ANY] * 8 + [VMEM] * 3,
        out_specs=[PER_SLOT] * 4 + [ANY] * 5,
        out_shape=[SLOT_SHAPE] * 4 + fold_shapes(3, True),
        scratch_shapes=[pltpu.VMEM((2, 2, 3, 3, N, N), F32), BLOCKS(3), pltpu.SemaphoreType.DMA((2, N_IN))],
        compiler_params=PARAMS,
    )(*scalars, *sides, probe, prop, prop_t)
    return out[:3], out[3], out[4:]


def turn(scalars, sides, incident, target, prop, prop_t, dft, dft_t):
    def kernel(offs, count, *rest):
        arrays, (wave_ref, target_ref, prop, prop_t, dft, dft_t) = rest[:8], rest[8:14]
        back_ref, parts = rest[14], rest[15:20]
        padded, totals, kept, sems = rest[20:]
        j = pl.program_id(0)
        fills = [copies_of(fill_pairs(padded.at[k], k + 2, k, *arrays), sems.at[k]) for k in range(2)]

        @pl.when(j == 0)
        def _():
            start_all(fills[0])
            start_all(fills[1])
            totals[...] = jnp.zeros_like(totals)
            wait_all(fills[0])

        @pl.when(j < count[0, 0])
        def _():
            place = Place(offs, j)
            window = window_of(padded.at[0], place)
            kept[0, 0], kept[0, 1] = window
            wave = both_axes(product_of(wave_in(wave_ref), window), prop, prop_t, True, True)
            kept[1, 0], kept[1, 1] = wave
            place.add(totals, 4, intensity(wave))

        @pl.when(j == 0)
        def _():
            wait_all(fills[1])

        @pl.when(j < count[0, 0])
        def _():
            place = Place(offs, j)
            window = window_of(padded.at[1], place)
            wave = (kept[1, 0], kept[1, 1])
            far = both_axes(product_of(wave, window), dft, dft_t, True, False)
            misfit = intensity(far) - target_ref[0]
            back = both_axes((misfit * far[0], misfit * far[1]), dft_t, dft, False, True)
            grad = conj_product(wave, back)
            place.add(totals, 0, grad[0])
            place.add(totals, 1, grad[1])
            back = both_axes(conj_product(window, back), prop_t, prop, True, True)
            grad = conj_product(wave_in(wave_ref), back)
            place.add(totals, 2, grad[0])
            place.add(totals, 3, grad[1])
            back = both_axes(conj_product((kept[0, 0], kept[0, 1]), back), prop_t, prop, True, True)
            put_wave(back_ref, back)

        @pl.when(j == SLOTS - 1)
        def _():
            drains = copies_of(drain_pairs(totals, 0, 5, False, *parts), sems.at[0])
            start_all(drains)
            wait_all(drains)

    out = pl.pallas_call(
        kernel,
        name="turn",
        grid=(SLOTS,),
        in_specs=[SMEM, SMEM] + [ANY] * 8 + [PER_SLOT, pl.BlockSpec((1, N, N), lambda j: (j, 0, 0))] + [VMEM] * 4,
        out_specs=[PER_SLOT] + [ANY] * 5,
        out_shape=[SLOT_SHAPE] + fold_shapes(5),
        scratch_shapes=[
            pltpu.VMEM((2, 2, 3, 3, N, N), F32),
            BLOCKS(5),
            pltpu.VMEM((2, 2, N, N), F32),
            pltpu.SemaphoreType.DMA((2, N_IN)),
        ],
        compiler_params=PARAMS,
    )(*scalars, *sides, incident, target, prop, prop_t, dft, dft_t)
    return out[0], out[1:]


def leave(scalars, incident_0, incident_1, window_1, back, prop, prop_t):
    def kernel(offs, count, wave_0, wave_1, window_ref, back_ref, prop, prop_t, *rest):
        parts, (totals, sems) = rest[:5], rest[5:]
        j = pl.program_id(0)

        @pl.when(j == 0)
        def _():
            totals[...] = jnp.zeros_like(totals)

        @pl.when(j < count[0, 0])
        def _():
            place = Place(offs, j)
            back = wave_in(back_ref)
            grad = conj_product(wave_in(wave_1), back)
            place.add(totals, 0, grad[0])
            place.add(totals, 1, grad[1])
            back = both_axes(conj_product(wave_in(window_ref), back), prop_t, prop, True, True)
            grad = conj_product(wave_in(wave_0), back)
            place.add(totals, 2, grad[0])
            place.add(totals, 3, grad[1])

        @pl.when(j == SLOTS - 1)
        def _():
            drains = copies_of(drain_pairs(totals, 0, 4, False, *parts), sems)
            start_all(drains)
            wait_all(drains)

    return pl.pallas_call(
        kernel,
        name="leave",
        grid=(SLOTS,),
        in_specs=[SMEM, SMEM] + [PER_SLOT] * 4 + [VMEM] * 2,
        out_specs=[ANY] * 5,
        out_shape=fold_shapes(4),
        scratch_shapes=[BLOCKS(4), pltpu.SemaphoreType.DMA((N_IN,))],
        compiler_params=PARAMS,
    )(*scalars, incident_0, incident_1, window_1, back, prop, prop_t)


def reorder_targets(measured):
    def kernel(m_ref, o_ref):
        r = lax.broadcasted_iota(jnp.int32, (N, N), 0)
        c = lax.broadcasted_iota(jnp.int32, (N, N), 1)

        def one_hot(to, source):
            return jnp.where(source == jnp.where(to < H, 2 * to, 2 * to - (N - 1)), 1.0, 0.0).astype(BF16)

        def thirds(x):
            a = x.astype(BF16)
            rest = x - a.astype(F32)
            b = rest.astype(BF16)
            return a, b, (rest - b.astype(F32)).astype(BF16)

        rows, cols = one_hot(r, c), one_hot(c, r)
        a, b, d = thirds(m_ref[0, 0, 0])
        x = (dot(rows, a) + dot(rows, b)) + dot(rows, d)
        a, b, d = thirds(x)
        o_ref[0] = (dot(a, cols) + dot(b, cols)) + dot(d, cols)

    return pl.pallas_call(
        kernel,
        name="reorder",
        grid=(SLOTS,),
        in_specs=[pl.BlockSpec((1, 1, 1, N, N), lambda j: (0, 0, j, 0, 0))],
        out_specs=pl.BlockSpec((1, N, N), lambda j: (j, 0, 0)),
        out_shape=jax.ShapeDtypeStruct((SLOTS, N, N), F32),
        compiler_params=PARAMS,
    )(measured)


def rims_with_rows(parts, from_above, from_below):
    left, right = parts[3:]
    planes = left.shape[0]

    def kernel(l_ref, r_ref, fal, far, fbl, fbr, lo, ro):
        for source, out, fa, fb in ((l_ref, lo, fal, fbl), (r_ref, ro, far, fbr)):
            out[:, :H, :] = source[:, :H, :] + fa[...]
            out[:, H:TILE - H, :] = source[:, H:TILE - H, :]
            out[:, TILE - H:, :] = source[:, TILE - H:, :] + fb[...]

    whole = pl.BlockSpec((planes, TILE, H), lambda i: (0, 0, 0))
    ends = [pl.BlockSpec((planes, H, H), lambda i: (0, 0, 0)), pl.BlockSpec((planes, H, H), lambda i: (0, 0, 5))]
    return pl.pallas_call(
        kernel,
        grid=(1,),
        in_specs=[whole] * 2 + ends * 2,
        out_specs=[whole] * 2,
        out_shape=[jax.ShapeDtypeStruct((planes, TILE, H), F32)] * 2,
    )(left, right, from_above, from_above, from_below, from_below)


def rims_with_columns(parts, from_left, from_right):
    top, bottom = parts[1:3]
    planes = top.shape[0]

    def kernel(t_ref, b_ref, flt, flb, frt, frb, to, bo):
        for source, out, fl, fr in ((t_ref, to, flt, frt), (b_ref, bo, flb, frb)):
            out[:, :, :H] = source[:, :, :H] + fl[...]
            out[:, :, H:TILE - H] = source[:, :, H:TILE - H]
            out[:, :, TILE - H:] = source[:, :, TILE - H:] + fr[...]

    whole = pl.BlockSpec((planes, H, TILE), lambda i: (0, 0, 0))
    ends = [pl.BlockSpec((planes, H, H), lambda i: (0, 0, 0)), pl.BlockSpec((planes, H, H), lambda i: (0, 5, 0))]
    return pl.pallas_call(
        kernel,
        name="light_rims",
        grid=(1,),
        in_specs=[whole] * 2 + ends * 2,
        out_specs=[whole] * 2,
        out_shape=[jax.ShapeDtypeStruct((planes, H, TILE), F32)] * 2,
    )(top, bottom, from_left, from_left, from_right, from_right)


def shifted(value, axis, steps):
    count = lax.axis_size(axis)
    leading, last = max(0, -steps), min(count, count - steps)
    return lax.ppermute(value, axis, [(source, source + steps) for source in range(leading, last)])


def light_scale(centre, from_left, from_right, from_above, from_below):
    planes, blocks = centre.shape[0], TILE // H

    def kernel(centre, left, right, above, below, out):
        c = pl.program_id(0)
        out[...] = centre[...]
        out[:, :H, :] += above[...]
        out[:, TILE - H:, :] += below[...]

        @pl.when(c == 0)
        def _():
            out[...] += left[:, H:H + TILE, :]

        @pl.when(c == blocks - 1)
        def _():
            out[...] += right[:, H:H + TILE, :]

        out[...] = 1.0 / (out[...] + 1.0)

    column = pl.BlockSpec((planes, TILE, H), lambda c: (0, 0, c))
    side = pl.BlockSpec((planes, 3 * N, H), lambda c: (0, 0, 0))
    end = pl.BlockSpec((planes, H, H), lambda c: (0, 0, c))
    return pl.pallas_call(
        kernel,
        name="light_scale",
        grid=(blocks,),
        in_specs=[column, side, side, end, end],
        out_specs=column,
        out_shape=jax.ShapeDtypeStruct((planes, TILE, TILE), F32),
        compiler_params=PARAMS,
    )(centre, from_left, from_right, from_above, from_below)


def update(slices, columns, amp, ph, centre, above, below, sides, scale, light_plane, previous, pair=0):
    base, stride = columns[0], (columns[1] - columns[0])
    touches = {0, 3} & set(columns)
    top_slice = slices[0]
    operands = [amp, ph, centre, above, below]
    column = lambda n, at: pl.BlockSpec((n, TILE, H), at)
    end = lambda n, at: pl.BlockSpec((n, H, H), at)
    of = lambda i: base + stride * i
    here = column(1, lambda a, i: (top_slice - a, 0, of(i)))
    specs = [here, here, column(2, lambda a, i: (a + pair, 0, of(i)))]
    specs += [end(2, lambda a, i: (a + pair, 0, of(i) + 1))] * 2
    if touches:
        operands += list(sides)
        specs += [column(2, lambda a, i: (a + pair, 0, 0))] * 2
    if light_plane is None:
        operands.append(scale)
        specs.append(column(1, lambda a, i: (top_slice - a, 0, of(i))))
    else:
        p = light_plane
        operands += [centre, above, below]
        specs += [column(1, lambda a, i: (p, 0, of(i)))] + [end(1, lambda a, i: (p, 0, of(i) + 1))] * 2
        if touches:
            operands += list(sides)
            specs += [column(1, lambda a, i: (p, 0, 0))] * 2
    used = len(operands)
    if previous:
        operands += list(previous)
        specs += [ANY] * 2

    def kernel(*refs):
        refs = list(refs)
        take = lambda: refs.pop(0)
        amp_ref, ph_ref = take(), take()
        c = of(pl.program_id(1))

        def total(p, parts):
            x = parts[0][p]
            x = jnp.concatenate([x[:H] + parts[1][p], x[H:TILE - H], x[TILE - H:] + parts[2][p]], 0)
            return x + side_of(c, parts[3][p], parts[4][p]) if touches else x

        grads = [take() for _ in range(5 if touches else 3)]
        if light_plane is None:
            scale = take()[0]
        else:
            scale = 1.0 / (total(0, [take() for _ in range(5 if touches else 3)]) + 1.0)
        out_r, out_i = refs[-2:]
        sine, cosine = sincos(ph_ref[0])
        out_r[0] = amp_ref[0] * cosine - total(0, grads) * scale
        out_i[0] = amp_ref[0] * sine - total(1, grads) * scale

    shape = jax.ShapeDtypeStruct((SLICES, TILE, TILE), F32)
    return pl.pallas_call(
        kernel,
        grid=(len(slices), len(columns)),
        in_specs=specs,
        out_specs=[here, here],
        out_shape=[shape, shape],
        input_output_aliases={used: 0, used + 1: 1} if previous else {},
        compiler_params=pltpu.CompilerParams(dimension_semantics=("arbitrary", "arbitrary")),
    )(*operands)


def side_of(c, left, right):
    return jnp.where(c == 0, left, jnp.where(c == TILE // H - 1, right, 0.0))


def program(object_amp, object_phase, probe_field, measured, offsets, counts):
    prop, dft = lax.optimization_barrier(tuple(jnp.asarray(t) for t in tables()))
    prop_t, dft_t = jnp.swapaxes(prop, 2, 3), jnp.swapaxes(dft, 2, 3)
    amp, ph = object_amp, object_phase
    scalars = (offsets, counts)
    edges = []
    for a, b in ((0, 2), (2, 4)):
        edge = lambda cols: jnp.stack([amp[a:b, :, cols], ph[a:b, :, cols]])
        left = shifted(edge(slice(TILE - H, TILE)), "col", 1)
        right = shifted(edge(slice(0, H)), "col", -1)
        edges.append((left, right))
    above = shifted(jnp.stack([amp[:, TILE - H:], ph[:, TILE - H:]]), "row", 1)
    below = shifted(jnp.stack([amp[:, :H], ph[:, :H]]), "row", -1)
    sides = []
    for left, right in edges:
        corner = lambda rows: jnp.concatenate([left[:, :, rows], right[:, :, rows]], 3)
        corner_a = shifted(corner(slice(TILE - H, TILE)), "row", 1)
        corner_b = shifted(corner(slice(0, H)), "row", -1)
        sides.append((amp, ph, left, right, above, below, corner_a, corner_b))
    target = reorder_targets(measured)

    waves, window_1, lights = enter(scalars, sides[0], probe_field, prop, prop_t)
    light_left = shifted(lights[4], "col", 1)
    light_right = shifted(lights[3], "col", -1)

    back, grads_a = turn(scalars, sides[1], waves[2], target, prop, prop_t, dft, dft_t)
    a_above = shifted(grads_a[2], "row", 1)
    a_below = shifted(grads_a[1], "row", -1)

    grads_b = leave(scalars, waves[0], waves[1], window_1, back, prop, prop_t)
    b_above = shifted(grads_b[2], "row", 1)
    b_below = shifted(grads_b[1], "row", -1)

    to_up, to_down = rims_with_columns(lights, light_left, light_right)
    light_above = shifted(to_down, "row", 1)
    light_below = shifted(to_up, "row", -1)

    to_left, to_right = rims_with_rows(grads_a, a_above, a_below)
    a_sides = shifted(to_right, "col", 1), shifted(to_left, "col", -1)
    scale = light_scale(lights[0], light_left, light_right, light_above, light_below)

    to_left, to_right = rims_with_rows(grads_b, b_above, b_below)
    b_sides = shifted(to_right, "col", 1), shifted(to_left, "col", -1)

    every, middle, ends = (0, 1, 2, 3), (1, 2), (0, 3)
    a_parts, b_parts = (grads_a[0], a_above, a_below), (grads_b[0], b_above, b_below)
    outs = update((1, 0), middle, amp, ph, *b_parts, None, scale, None, None)
    outs = update((3,), every, amp, ph, *a_parts, a_sides, None, 4, outs)
    outs = update((2,), every, amp, ph, *a_parts, a_sides, scale, None, outs, pair=1)
    outs = update((1, 0), ends, amp, ph, *b_parts, b_sides, scale, None, outs)
    return tuple(outs)


def solution(mesh):
    placed = (
        P(None, "row", "col"),
        P(None, "row", "col"),
        P(),
        P("row", "col", None, None, None),
        P("row", "col", None, None),
        P("row", "col"),
    )
    return jax.shard_map(
        program,
        mesh=mesh,
        in_specs=placed,
        out_specs=(P(None, "row", "col"), P(None, "row", "col")),
        check_vma=False,
    )
```

profile of v0, /device:TPU:49, one launch (start us, length us, event | category | flops | bytes accessed | tf_op | source)
XLA Modules:
  0.0 239.5 jit_solution(7569619260433973642)
XLA Ops:
  0.6 2.7 %slice_bitcast_fusion.4 = (f32[1,2,512,128]{3,2,1,0:T(8,128)S(1)}, f32[1,2,512,128]{3,2,1,0:T(8,128)S(1)}, f32[1,2,512,128]{3,2,1,0:T(8,128)S(1)}, f32[1,2,512,1...) fusion(f32[4,512,512]{2,1,0:T(8,128)} %refs_1_.7, ...), kind=kLoop, calls=%fused_computation.14 | loop fusion | bytes 8388608 | tf_op jit(solution)/shard_map/stack | solution.py:588
  3.4 3.8 %collective-permute-start = (f32[2,2,512,128]{3,2,1,0:T(8,128)S(1)}, f32[2,2,512,128]{3,2,1,0:T(8,128)S(1)}, u32[]{:S(2)}, u32[]{:S(2)}) collective-permute-start(f32[2,2,512,128]{3,2,1,0:T(8,128)S(1)} %pad_maximum_fusion.2), channel_id=1, source_target_pairs={{0,1},{1,2},{2,3},{3,4},{4,5},{5,6},{6,7},{7,8},{8,9},{9,10},{10,1... | collective-permute-start | bytes 3145736 | tf_op jit(solution)/shard_map/ppermute | solution.py:479
  7.3 1.9 collective-permute-start.1
  9.8 1.6 pad_maximum_fusion
  11.5 3.9 %collective-permute-start.2 = (f32[2,4,128,512]{3,2,1,0:T(8,128)}, f32[2,4,128,512]{3,2,1,0:T(8,128)S(1)}, u32[]{:S(2)}, u32[]{:S(2)}) collective-permute-start(f32[2,4,128,512]{3,2,1,0:T(8,128)} %pad_maximum_fusion), channel_id=1, source_target_pairs={{0,16},{16,32},{32,48},{48,64},{64,80},{80,96},{96,112},{1,17},{17... | collective-permute-start | bytes 6291464 | tf_op jit(solution)/shard_map/ppermute | solution.py:479
  15.4 1.6 pad_maximum_fusion.1
  17.0 1.9 collective-permute-start.3
  19.0 3.5 %collective-permute-start.6 = (f32[2,2,512,128]{3,2,1,0:T(8,128)S(1)}, f32[2,2,512,128]{3,2,1,0:T(8,128)S(1)}, u32[]{:S(2)}, u32[]{:S(2)}) collective-permute-start(f32[2,2,512,128]{3,2,1,0:T(8,128)S(1)} %pad_maximum_fusion.4), channel_id=1, source_target_pairs={{0,1},{1,2},{2,3},{3,4},{4,5},{5,6},{6,7},{7,8},{8,9},{9,10},{10,1... | collective-permute-start | bytes 3145736 | tf_op jit(solution)/shard_map/ppermute | solution.py:479
  22.6 7.0 %collective-permute-done.rest_2_ = f32[2,2,512,128]{3,2,1,0:T(8,128)S(1)} collective-permute-done((f32[2,2,512,128]{3,2,1,0:T(8,128)S(1)}, f32[2,2,512,128]{3,2,1,0:T(8,128)S(1)}, u32[]{:S(2)}, u32[]{:S(2)}) %collective-permute-start) | collective-permute-done | bytes 1048608 | tf_op jit(solution)/shard_map/ppermute | solution.py:479
  29.6 1.9 collective-permute-start.7
  33.0 4.7 %collective-permute-start.4 = (f32[2,2,128,256]{3,2,1,0:T(8,128)S(1)}, f32[2,2,128,256]{3,2,1,0:T(8,128)S(1)}, u32[]{:S(2)}, u32[]{:S(2)}) collective-permute-start(f32[2,2,128,256]{3,2,1,0:T(8,128)S(1)} %pad_maximum_fusion.6), channel_id=1, source_target_pairs={{0,16},{16,32},{32,48},{48,64},{64,80},{80,96},{96,112},{1,17},{17... | collective-permute-start | bytes 1572872 | tf_op jit(solution)/shard_map/ppermute | solution.py:479
  38.6 13.4 %collective-permute-done.6.rest_2_ = f32[2,2,512,128]{3,2,1,0:T(8,128)S(1)} collective-permute-done((f32[2,2,512,128]{3,2,1,0:T(8,128)S(1)}, f32[2,2,512,128]{3,2,1,0:T(8,128)S(1)}, u32[]{:S(2)}, u32[]{:S(2)}) %collective-permute-start.6) | collective-permute-done | bytes 1048608 | tf_op jit(solution)/shard_map/ppermute | solution.py:479
  52.1 3.4 %collective-permute-start.5 = (f32[2,2,128,256]{3,2,1,0:T(8,128)}, f32[2,2,128,256]{3,2,1,0:T(8,128)}, u32[]{:S(2)}, u32[]{:S(2)}) collective-permute-start(f32[2,2,128,256]{3,2,1,0:T(8,128)} %pad_maximum_fusion.7), channel_id=1, source_target_pairs={{16,0},{32,16},{48,32},{64,48},{80,64},{96,80},{112,96},{17,1},{33... | collective-permute-start | bytes 1572872 | tf_op jit(solution)/shard_map/ppermute | solution.py:479
  56.6 4.4 %collective-permute-start.8 = (f32[2,2,128,256]{3,2,1,0:T(8,128)}, f32[2,2,128,256]{3,2,1,0:T(8,128)}, u32[]{:S(2)}, u32[]{:S(2)}) collective-permute-start(f32[2,2,128,256]{3,2,1,0:T(8,128)} %pad_maximum_fusion.8), channel_id=1, source_target_pairs={{0,16},{16,32},{32,48},{48,64},{64,80},{80,96},{96,112},{1,17},{17... | collective-permute-start | bytes 1572872 | tf_op jit(solution)/shard_map/ppermute | solution.py:479
  61.8 1.9 collective-permute-start.9
  64.5 1.0 copy.17.rest_9_.rest_10_.prop
  65.5 1.3 copy-done.5
  66.8 15.6 %enter.1 = (f32[4,2,256,256]{3,2,1,0:T(8,128)}, f32[4,2,256,256]{3,2,1,0:T(8,128)}, f32[4,2,256,256]{3,2,1,0:T(8,128)}, f32[4,2,256,256]{3,2,1,0:T(8,128)}, f32[...) custom-call(s32[1,1,4,2]{3,2,1,0:T(4,128)} %copy.21.offs, ...), custom_call_target="tpu_custom_call" | custom-call | tf_op jit(solution)/shard_map/enter/pallas_call | solution.py:280
  82.4 7.8 %collective-permute-start.14 = (f32[3,768,128]{2,1,0:T(8,128)}, f32[3,768,128]{2,1,0:T(8,128)}, u32[]{:S(2)}, u32[]{:S(2)}) collective-permute-start(f32[3,768,128]{2,1,0:T(8,128)} %get-tuple-element.51), channel_id=1, source_target_pairs={{0,1},{1,2},{2,3},{3,4},{4,5},{5,6},{6,7},{7,8},{8,9},{9,10},{10,1... | collective-permute-start | bytes 3538952 | tf_op jit(solution)/shard_map/ppermute | solution.py:479
  90.3 1.0 copy.20.rest_12_
  91.3 4.6 %reorder.1.rest_9_ = f32[4,256,256]{2,1,0:T(8,128)} custom-call(f32[1,1,4,256,256]{4,3,2,1,0:T(8,128)} %m_ref.1), custom_call_target="tpu_custom_call" | custom-call | tf_op jit(solution)/shard_map/reorder/pallas_call | solution.py:422
  95.9 21.7 %turn.1 = (f32[4,2,256,256]{3,2,1,0:T(8,128)}, f32[5,512,512]{2,1,0:T(8,128)}, f32[5,128,768]{2,1,0:T(8,128)}, f32[5,128,768]{2,1,0:T(8,128)}, f32[5,512,128]{2,1,0:T(8,128)}, /*index=5*/f32[5,512,128]{2,1,0:T(8,128)}) custom-call(s32[1,1,4,2]{3,2,1,0:T(4,128)} %copy.21.offs, s32[1,1]{1,0:T(1,128)S(6)} %copy.29.count, f32[4,512,512]{2,1,0:T(8,128)} %refs_0_.7, ...), custom_call_target="tpu_custom_call" | custom-call | tf_op jit(solution)/shard_map/turn/pallas_call | solution.py:345
  117.7 3.7 %collective-permute-start.18 = (f32[5,128,768]{2,1,0:T(8,128)}, f32[5,128,768]{2,1,0:T(8,128)S(1)}, u32[]{:S(2)}, u32[]{:S(2)}) collective-permute-start(f32[5,128,768]{2,1,0:T(8,128)} %get-tuple-element.58), channel_id=1, source_target_pairs={{0,16},{16,32},{32,48},{48,64},{64,80},{80,96},{96,112},{1,17},{17... | collective-permute-start | bytes 5898248 | tf_op jit(solution)/shard_map/ppermute | solution.py:479
  121.4 2.7 %collective-permute-start.19 = (f32[5,128,768]{2,1,0:T(8,128)}, f32[5,128,768]{2,1,0:T(8,128)}, u32[]{:S(2)}, u32[]{:S(2)}) collective-permute-start(f32[5,128,768]{2,1,0:T(8,128)} %get-tuple-element.59), channel_id=1, source_target_pairs={{16,0},{32,16},{48,32},{64,48},{80,64},{96,80},{112,96},{17,1},{33... | collective-permute-start | bytes 5898248 | tf_op jit(solution)/shard_map/ppermute | solution.py:479
  124.1 8.6 %collective-permute-start.15 = (f32[3,768,128]{2,1,0:T(8,128)}, f32[3,768,128]{2,1,0:T(8,128)}, u32[]{:S(2)}, u32[]{:S(2)}) collective-permute-start(f32[3,768,128]{2,1,0:T(8,128)} %get-tuple-element.52), channel_id=1, source_target_pairs={{1,0},{2,1},{3,2},{4,3},{5,4},{6,5},{7,6},{8,7},{9,8},{10,9},{11,1... | collective-permute-start | bytes 3538952 | tf_op jit(solution)/shard_map/ppermute | solution.py:479
  132.7 11.1 %leave.1 = (f32[4,512,512]{2,1,0:T(8,128)}, f32[4,128,768]{2,1,0:T(8,128)}, f32[4,128,768]{2,1,0:T(8,128)}, f32[4,512,128]{2,1,0:T(8,128)}, f32[4,512,128]{2,1,0:T(8,128)}) custom-call(s32[1,1,4,2]{3,2,1,0:T(4,128)} %copy.21.offs, s32[1,1]{1,0:T(1,128)S(6)} %copy.29.count, f32[4,2,256,256]{3,2,1,0:T(8,128)} %get-tuple-element.37.wave_0, ...), custom_call_target="tpu_custom_call" | custom-call | tf_op jit(solution)/shard_map/leave/pallas_call | solution.py:390
  143.9 3.9 %collective-permute-start.10 = (f32[4,128,768]{2,1,0:T(8,128)}, f32[4,128,768]{2,1,0:T(8,128)S(1)}, u32[]{:S(2)}, u32[]{:S(2)}) collective-permute-start(f32[4,128,768]{2,1,0:T(8,128)} %get-tuple-element.44), channel_id=1, source_target_pairs={{0,16},{16,32},{32,48},{48,64},{64,80},{80,96},{96,112},{1,17},{17... | collective-permute-start | bytes 4718600 | tf_op jit(solution)/shard_map/ppermute | solution.py:479
  147.8 1.9 collective-permute-start.11
  149.8 12.8 %collective-permute-done.15.frt.frb.right = f32[3,768,128]{2,1,0:T(8,128)} collective-permute-done((f32[3,768,128]{2,1,0:T(8,128)}, f32[3,768,128]{2,1,0:T(8,128)}, u32[]{:S(2)}, u32[]{:S(2)}) %collective-permute-start.15) | collective-permute-done | bytes 1179680 | tf_op jit(solution)/shard_map/ppermute | solution.py:479
  162.6 2.8 %light_rims.1 = (f32[3,128,512]{2,1,0:T(8,128)}, f32[3,128,512]{2,1,0:T(8,128)}) custom-call(f32[3,128,512]{2,1,0:T(8,128)} %get-tuple-element.53.t_ref, f32[3,128,512]{2,1,0:T(8,128)} %get-tuple-element.54.b_ref, f32[3,768,128]{2,1,0:T(8,128)} %collective-permute-done.14.flt.flb.left, f32[3,768,128]{2,1,0:T(8,128)} %collective-permute-done.14.flt.flb.left, ...), custom_call_target="tpu_custom_call" | custom-call | tf_op jit(solution)/shard_map/light_rims/pallas_call | solution.py:466
  165.4 1.9 collective-permute-start.16
  167.4 1.2 copy-done.2
  168.6 3.7 %shard_map.96 = (f32[5,512,128]{2,1,0:T(8,128)}, f32[5,512,128]{2,1,0:T(8,128)}) custom-call(f32[5,512,128]{2,1,0:T(8,128)} %get-tuple-element.60.l_ref, f32[5,512,128]{2,1,0:T(8,128)} %get-tuple-element.61.r_ref, f32[5,128,768]{2,1,0:T(8,128)} %copy-done.2, f32[5,128,768]{2,1,0:T(8,128)} %copy-done.2, ...), custom_call_target="tpu_custom_call" | custom-call | tf_op jit(solution)/shard_map/pallas_call | solution.py:445
  172.3 4.7 %collective-permute-start.20 = (f32[5,512,128]{2,1,0:T(8,128)}, f32[5,512,128]{2,1,0:T(8,128)S(1)}, u32[]{:S(2)}, u32[]{:S(2)}) collective-permute-start(f32[5,512,128]{2,1,0:T(8,128)} %get-tuple-element.62), channel_id=1, source_target_pairs={{0,1},{1,2},{2,3},{3,4},{4,5},{5,6},{6,7},{7,8},{8,9},{9,10},{10,1... | collective-permute-start | bytes 3932168 | tf_op jit(solution)/shard_map/ppermute | solution.py:479
  177.0 1.9 collective-permute-start.21
  179.0 1.2 copy-done.3
  180.2 3.2 %shard_map.95 = (f32[4,512,128]{2,1,0:T(8,128)}, f32[4,512,128]{2,1,0:T(8,128)}) custom-call(f32[4,512,128]{2,1,0:T(8,128)} %get-tuple-element.46.l_ref, f32[4,512,128]{2,1,0:T(8,128)} %get-tuple-element.47.r_ref, f32[4,128,768]{2,1,0:T(8,128)} %copy-done.3, f32[4,128,768]{2,1,0:T(8,128)} %copy-done.3, ...), custom_call_target="tpu_custom_call" | custom-call | tf_op jit(solution)/shard_map/pallas_call | solution.py:445
  183.4 4.4 %collective-permute-start.12 = (f32[4,512,128]{2,1,0:T(8,128)}, f32[4,512,128]{2,1,0:T(8,128)S(1)}, u32[]{:S(2)}, u32[]{:S(2)}) collective-permute-start(f32[4,512,128]{2,1,0:T(8,128)} %get-tuple-element.48), channel_id=1, source_target_pairs={{0,1},{1,2},{2,3},{3,4},{4,5},{5,6},{6,7},{7,8},{8,9},{9,10},{10,1... | collective-permute-start | bytes 3145736 | tf_op jit(solution)/shard_map/ppermute | solution.py:479
  187.8 1.9 collective-permute-start.13
  189.8 1.9 collective-permute-start.17
  191.7 12.0 %collective-permute-done.17.below = f32[3,128,512]{2,1,0:T(8,128)} collective-permute-done((f32[3,128,512]{2,1,0:T(8,128)}, f32[3,128,512]{2,1,0:T(8,128)}, u32[]{:S(2)}, u32[]{:S(2)}) %collective-permute-start.17) | collective-permute-done | bytes 786464 | tf_op jit(solution)/shard_map/ppermute | solution.py:479
  203.7 5.9 %light_scale.1.refs_5_.refs_7_ = f32[3,512,512]{2,1,0:T(8,128)} custom-call(f32[3,512,512]{2,1,0:T(8,128)} %get-tuple-element.50.centre, f32[3,768,128]{2,1,0:T(8,128)} %collective-permute-done.14.flt.flb.left, f32[3,768,128]{2,1,0:T(8,128)} %collective-permute-done.15.frt.frb.right, f32[3,128,512]{2,1,0:T(8,128)} %collective-permute-done.16.above, ...), custom_call_target="tpu_custom_call" | custom-call | tf_op jit(solution)/shard_map/light_scale/pallas_call | solution.py:504
  209.6 5.0 %shard_map.97 = (f32[4,512,512]{2,1,0:T(8,128)}, f32[4,512,512]{2,1,0:T(8,128)}) custom-call(f32[4,512,512]{2,1,0:T(8,128)} %refs_0_.7, f32[4,512,512]{2,1,0:T(8,128)} %refs_1_.7, f32[4,512,512]{2,1,0:T(8,128)} %get-tuple-element.43.refs_2_, f32[4,128,768]{2,1,0:T(8,128)} %copy-done.3, f32[4,128,768]{2,1,0:T(8,128)} %collective-permute-done.11.fbl.fbr.refs_4_, ...), custom_call_target="tpu_custom_call" | custom-call | tf_op jit(solution)/shard_map/pallas_call | solution.py:566
  214.6 1.0 copy-done.4
  215.7 6.0 %shard_map.98 = (f32[4,512,512]{2,1,0:T(8,128)}, f32[4,512,512]{2,1,0:T(8,128)}) custom-call(f32[4,512,512]{2,1,0:T(8,128)} %refs_0_.7, f32[4,512,512]{2,1,0:T(8,128)} %refs_1_.7, f32[5,512,512]{2,1,0:T(8,128)} %get-tuple-element.57.refs_2_.refs_7_, f32[5,128,768]{2,1,0:T(8,128)} %copy-done.2, ...), custom_call_target="tpu_custom_call", output_to_operand_aliasing={{0}: (12, {}), {1}: (13, {})} | custom-call | tf_op jit(solution)/shard_map/pallas_call | solution.py:566
  221.7 5.6 %shard_map.99 = (f32[4,512,512]{2,1,0:T(8,128)}, f32[4,512,512]{2,1,0:T(8,128)}) custom-call(f32[4,512,512]{2,1,0:T(8,128)} %refs_0_.7, f32[4,512,512]{2,1,0:T(8,128)} %refs_1_.7, f32[5,512,512]{2,1,0:T(8,128)} %get-tuple-element.57.refs_2_.refs_7_, f32[5,128,768]{2,1,0:T(8,128)} %copy-done.2, ...), custom_call_target="tpu_custom_call", output_to_operand_aliasing={{0}: (8, {}), {1}: (9, {})} | custom-call | tf_op jit(solution)/shard_map/pallas_call | solution.py:566
  228.1 4.7 %collective-permute-done.13.refs_6_ = f32[4,512,128]{2,1,0:T(8,128)S(1)} collective-permute-done((f32[4,512,128]{2,1,0:T(8,128)}, f32[4,512,128]{2,1,0:T(8,128)S(1)}, u32[]{:S(2)}, u32[]{:S(2)}) %collective-permute-start.13) | collective-permute-done | bytes 1048608 | tf_op jit(solution)/shard_map/ppermute | solution.py:479
  233.8 5.7 %shard_map.100 = (f32[4,512,512]{2,1,0:T(8,128)}, f32[4,512,512]{2,1,0:T(8,128)}) custom-call(f32[4,512,512]{2,1,0:T(8,128)} %refs_0_.7, f32[4,512,512]{2,1,0:T(8,128)} %refs_1_.7, f32[4,512,512]{2,1,0:T(8,128)} %get-tuple-element.43.refs_2_, f32[4,128,768]{2,1,0:T(8,128)} %copy-done.3, ...), custom_call_target="tpu_custom_call", output_to_operand_aliasing={{0}: (8, {}), {1}: (9, {})} | custom-call | tf_op jit(solution)/shard_map/pallas_call | solution.py:566
  (59 shorter events, 6.9 us)
Async XLA Ops:
  0.6 8.6 %copy-start.1 = (f32[4,512,512]{2,1,0:T(8,128)S(1)}, f32[4,512,512]{2,1,0:T(8,128)}, u32[]{:S(2)}) copy-start(f32[4,512,512]{2,1,0:T(8,128)} %refs_1_.7) | copy-start | bytes 12582916
  3.3 5.9 %copy-start = (f32[4,512,512]{2,1,0:T(8,128)S(1)}, f32[4,512,512]{2,1,0:T(8,128)}, u32[]{:S(2)}) copy-start(f32[4,512,512]{2,1,0:T(8,128)} %refs_0_.7) | copy-start | bytes 12582916
  3.4 26.2 %collective-permute-start = (f32[2,2,512,128]{3,2,1,0:T(8,128)S(1)}, f32[2,2,512,128]{3,2,1,0:T(8,128)S(1)}, u32[]{:S(2)}, u32[]{:S(2)}) collective-permute-start(f32[2,2,512,128]{3,2,1,0:T(8,128)S(1)} %pad_maximum_fusion.2), channel_id=1, source_target_pairs={{0,1},{1,2},{2,3},{3,4},{4,5},{5,6},{6,7},{7,8},{8,9},{9,10},{10,1... | collective-permute-start | bytes 3145736 | tf_op jit(solution)/shard_map/ppermute | solution.py:479
  7.3 25.7 %collective-permute-start.1 = (f32[2,2,512,128]{3,2,1,0:T(8,128)S(1)}, f32[2,2,512,128]{3,2,1,0:T(8,128)S(1)}, u32[]{:S(2)}, u32[]{:S(2)}) collective-permute-start(f32[2,2,512,128]{3,2,1,0:T(8,128)S(1)} %pad_maximum_fusion.3), channel_id=1, source_target_pairs={{1,0},{2,1},{3,2},{4,3},{5,4},{6,5},{7,6},{8,7},{9,8},{10,9},{11,1... | collective-permute-start | bytes 3145736 | tf_op jit(solution)/shard_map/ppermute | solution.py:479
  11.5 54.1 %collective-permute-start.2 = (f32[2,4,128,512]{3,2,1,0:T(8,128)}, f32[2,4,128,512]{3,2,1,0:T(8,128)S(1)}, u32[]{:S(2)}, u32[]{:S(2)}) collective-permute-start(f32[2,4,128,512]{3,2,1,0:T(8,128)} %pad_maximum_fusion), channel_id=1, source_target_pairs={{0,16},{16,32},{32,48},{48,64},{64,80},{80,96},{96,112},{1,17},{17... | collective-permute-start | bytes 6291464 | tf_op jit(solution)/shard_map/ppermute | solution.py:479
  17.0 48.5 %collective-permute-start.3 = (f32[2,4,128,512]{3,2,1,0:T(8,128)}, f32[2,4,128,512]{3,2,1,0:T(8,128)}, u32[]{:S(2)}, u32[]{:S(2)}) collective-permute-start(f32[2,4,128,512]{3,2,1,0:T(8,128)} %pad_maximum_fusion.1), channel_id=1, source_target_pairs={{16,0},{32,16},{48,32},{64,48},{80,64},{96,80},{112,96},{17,1},{33... | collective-permute-start | bytes 6291464 | tf_op jit(solution)/shard_map/ppermute | solution.py:479
  19.0 33.1 %collective-permute-start.6 = (f32[2,2,512,128]{3,2,1,0:T(8,128)S(1)}, f32[2,2,512,128]{3,2,1,0:T(8,128)S(1)}, u32[]{:S(2)}, u32[]{:S(2)}) collective-permute-start(f32[2,2,512,128]{3,2,1,0:T(8,128)S(1)} %pad_maximum_fusion.4), channel_id=1, source_target_pairs={{0,1},{1,2},{2,3},{3,4},{4,5},{5,6},{6,7},{7,8},{8,9},{9,10},{10,1... | collective-permute-start | bytes 3145736 | tf_op jit(solution)/shard_map/ppermute | solution.py:479
  29.6 9.0 %copy-start.9 = (f32[2,2,512,128]{3,2,1,0:T(8,128)}, f32[2,2,512,128]{3,2,1,0:T(8,128)S(1)}, u32[]{:S(2)}) copy-start(f32[2,2,512,128]{3,2,1,0:T(8,128)S(1)} %collective-permute-done.rest_2_) | copy-start | bytes 3145732
  29.6 26.0 %collective-permute-start.7 = (f32[2,2,512,128]{3,2,1,0:T(8,128)S(1)}, f32[2,2,512,128]{3,2,1,0:T(8,128)S(1)}, u32[]{:S(2)}, u32[]{:S(2)}) collective-permute-start(f32[2,2,512,128]{3,2,1,0:T(8,128)S(1)} %pad_maximum_fusion.5), channel_id=1, source_target_pairs={{1,0},{2,1},{3,2},{4,3},{5,4},{6,5},{7,6},{8,7},{9,8},{10,9},{11,1... | collective-permute-start | bytes 3145736 | tf_op jit(solution)/shard_map/ppermute | solution.py:479
  33.0 22.6 %copy-start.10 = (f32[2,2,512,128]{3,2,1,0:T(8,128)}, f32[2,2,512,128]{3,2,1,0:T(8,128)S(1)}, u32[]{:S(2)}) copy-start(f32[2,2,512,128]{3,2,1,0:T(8,128)S(1)} %collective-permute-done.1.rest_3_) | copy-start | bytes 3145732
  33.0 28.8 %collective-permute-start.4 = (f32[2,2,128,256]{3,2,1,0:T(8,128)S(1)}, f32[2,2,128,256]{3,2,1,0:T(8,128)S(1)}, u32[]{:S(2)}, u32[]{:S(2)}) collective-permute-start(f32[2,2,128,256]{3,2,1,0:T(8,128)S(1)} %pad_maximum_fusion.6), channel_id=1, source_target_pairs={{0,16},{16,32},{32,48},{48,64},{64,80},{80,96},{96,112},{1,17},{17... | collective-permute-start | bytes 1572872 | tf_op jit(solution)/shard_map/ppermute | solution.py:479
  38.6 25.2 %copy-start.15 = (s32[1,1,4,2]{2,3,1,0:T(2,128)S(1)}, s32[1,1,4,2]{2,3,1,0:T(2,128)}, u32[]{:S(2)}) copy-start(s32[1,1,4,2]{2,3,1,0:T(2,128)} %param.12) | copy-start | bytes 100
  38.6 25.9 %copy-start.6 = (bf16[2,2,256,256]{2,3,1,0:T(8,128)(2,1)S(1)}, bf16[2,2,256,256]{2,3,1,0:T(8,128)(2,1)}, u32[]{:S(2)}) copy-start(bf16[2,2,256,256]{2,3,1,0:T(8,128)(2,1)} %constant.4.clone) | copy-start | bytes 1572868
  52.1 9.8 %copy-start.7 = (f32[2,2,512,128]{3,2,1,0:T(8,128)}, f32[2,2,512,128]{3,2,1,0:T(8,128)S(1)}, u32[]{:S(2)}) copy-start(f32[2,2,512,128]{3,2,1,0:T(8,128)S(1)} %collective-permute-done.6.rest_2_) | copy-start | bytes 3145732
  52.1 13.4 %collective-permute-start.5 = (f32[2,2,128,256]{3,2,1,0:T(8,128)}, f32[2,2,128,256]{3,2,1,0:T(8,128)}, u32[]{:S(2)}, u32[]{:S(2)}) collective-permute-start(f32[2,2,128,256]{3,2,1,0:T(8,128)} %pad_maximum_fusion.7), channel_id=1, source_target_pairs={{16,0},{32,16},{48,32},{64,48},{80,64},{96,80},{112,96},{17,1},{33... | collective-permute-start | bytes 1572872 | tf_op jit(solution)/shard_map/ppermute | solution.py:479
  55.6 6.3 %copy-start.8 = (f32[2,2,512,128]{3,2,1,0:T(8,128)}, f32[2,2,512,128]{3,2,1,0:T(8,128)S(1)}, u32[]{:S(2)}) copy-start(f32[2,2,512,128]{3,2,1,0:T(8,128)S(1)} %collective-permute-done.7.rest_3_) | copy-start | bytes 3145732
  56.6 39.4 %collective-permute-start.8 = (f32[2,2,128,256]{3,2,1,0:T(8,128)}, f32[2,2,128,256]{3,2,1,0:T(8,128)}, u32[]{:S(2)}, u32[]{:S(2)}) collective-permute-start(f32[2,2,128,256]{3,2,1,0:T(8,128)} %pad_maximum_fusion.8), channel_id=1, source_target_pairs={{0,16},{16,32},{32,48},{48,64},{64,80},{80,96},{96,112},{1,17},{17... | collective-permute-start | bytes 1572872 | tf_op jit(solution)/shard_map/ppermute | solution.py:479
  61.8 3.7 %copy-start.14 = (f32[2,2,128,256]{3,2,1,0:T(8,128)}, f32[2,2,128,256]{3,2,1,0:T(8,128)S(1)}, u32[]{:S(2)}) copy-start(f32[2,2,128,256]{3,2,1,0:T(8,128)S(1)} %collective-permute-done.4.rest_6_) | copy-start | bytes 1572868
  61.8 34.1 %collective-permute-start.9 = (f32[2,2,128,256]{3,2,1,0:T(8,128)}, f32[2,2,128,256]{3,2,1,0:T(8,128)}, u32[]{:S(2)}, u32[]{:S(2)}) collective-permute-start(f32[2,2,128,256]{3,2,1,0:T(8,128)} %pad_maximum_fusion.9), channel_id=1, source_target_pairs={{16,0},{32,16},{48,32},{64,48},{80,64},{96,80},{112,96},{17,1},{33... | collective-permute-start | bytes 1572872 | tf_op jit(solution)/shard_map/ppermute | solution.py:479
  65.5 1.3 copy-start.5
  66.8 23.5 %copy-start.11 = (bf16[2,2,256,256]{2,3,1,0:T(8,128)(2,1)S(1)}, bf16[2,2,256,256]{2,3,1,0:T(8,128)(2,1)}, u32[]{:S(2)}) copy-start(bf16[2,2,256,256]{2,3,1,0:T(8,128)(2,1)} %constant.5.clone) | copy-start | bytes 1572868
  82.4 65.4 %collective-permute-start.14 = (f32[3,768,128]{2,1,0:T(8,128)}, f32[3,768,128]{2,1,0:T(8,128)}, u32[]{:S(2)}, u32[]{:S(2)}) collective-permute-start(f32[3,768,128]{2,1,0:T(8,128)} %get-tuple-element.51), channel_id=1, source_target_pairs={{0,1},{1,2},{2,3},{3,4},{4,5},{5,6},{6,7},{7,8},{8,9},{9,10},{10,1... | collective-permute-start | bytes 3538952 | tf_op jit(solution)/shard_map/ppermute | solution.py:479
  117.7 49.7 %collective-permute-start.18 = (f32[5,128,768]{2,1,0:T(8,128)}, f32[5,128,768]{2,1,0:T(8,128)S(1)}, u32[]{:S(2)}, u32[]{:S(2)}) collective-permute-start(f32[5,128,768]{2,1,0:T(8,128)} %get-tuple-element.58), channel_id=1, source_target_pairs={{0,16},{16,32},{32,48},{48,64},{64,80},{80,96},{96,112},{1,17},{17... | collective-permute-start | bytes 5898248 | tf_op jit(solution)/shard_map/ppermute | solution.py:479
  121.4 46.0 %collective-permute-start.19 = (f32[5,128,768]{2,1,0:T(8,128)}, f32[5,128,768]{2,1,0:T(8,128)}, u32[]{:S(2)}, u32[]{:S(2)}) collective-permute-start(f32[5,128,768]{2,1,0:T(8,128)} %get-tuple-element.59), channel_id=1, source_target_pairs={{16,0},{32,16},{48,32},{64,48},{80,64},{96,80},{112,96},{17,1},{33... | collective-permute-start | bytes 5898248 | tf_op jit(solution)/shard_map/ppermute | solution.py:479
  124.1 38.5 %collective-permute-start.15 = (f32[3,768,128]{2,1,0:T(8,128)}, f32[3,768,128]{2,1,0:T(8,128)}, u32[]{:S(2)}, u32[]{:S(2)}) collective-permute-start(f32[3,768,128]{2,1,0:T(8,128)} %get-tuple-element.52), channel_id=1, source_target_pairs={{1,0},{2,1},{3,2},{4,3},{5,4},{6,5},{7,6},{8,7},{9,8},{10,9},{11,1... | collective-permute-start | bytes 3538952 | tf_op jit(solution)/shard_map/ppermute | solution.py:479
  143.9 35.1 %collective-permute-start.10 = (f32[4,128,768]{2,1,0:T(8,128)}, f32[4,128,768]{2,1,0:T(8,128)S(1)}, u32[]{:S(2)}, u32[]{:S(2)}) collective-permute-start(f32[4,128,768]{2,1,0:T(8,128)} %get-tuple-element.44), channel_id=1, source_target_pairs={{0,16},{16,32},{32,48},{48,64},{64,80},{80,96},{96,112},{1,17},{17... | collective-permute-start | bytes 4718600 | tf_op jit(solution)/shard_map/ppermute | solution.py:479
  147.8 31.2 %collective-permute-start.11 = (f32[4,128,768]{2,1,0:T(8,128)}, f32[4,128,768]{2,1,0:T(8,128)}, u32[]{:S(2)}, u32[]{:S(2)}) collective-permute-start(f32[4,128,768]{2,1,0:T(8,128)} %get-tuple-element.45), channel_id=1, source_target_pairs={{16,0},{32,16},{48,32},{64,48},{80,64},{96,80},{112,96},{17,1},{33... | collective-permute-start | bytes 4718600 | tf_op jit(solution)/shard_map/ppermute | solution.py:479
  165.4 24.3 %collective-permute-start.16 = (f32[3,128,512]{2,1,0:T(8,128)}, f32[3,128,512]{2,1,0:T(8,128)}, u32[]{:S(2)}, u32[]{:S(2)}) collective-permute-start(f32[3,128,512]{2,1,0:T(8,128)} %get-tuple-element.55), channel_id=1, source_target_pairs={{0,16},{16,32},{32,48},{48,64},{64,80},{80,96},{96,112},{1,17},{17... | collective-permute-start | bytes 2359304 | tf_op jit(solution)/shard_map/ppermute | solution.py:479
  167.4 1.3 copy-start.2
  172.3 42.3 %collective-permute-start.20 = (f32[5,512,128]{2,1,0:T(8,128)}, f32[5,512,128]{2,1,0:T(8,128)S(1)}, u32[]{:S(2)}, u32[]{:S(2)}) collective-permute-start(f32[5,512,128]{2,1,0:T(8,128)} %get-tuple-element.62), channel_id=1, source_target_pairs={{0,1},{1,2},{2,3},{3,4},{4,5},{5,6},{6,7},{7,8},{8,9},{9,10},{10,1... | collective-permute-start | bytes 3932168 | tf_op jit(solution)/shard_map/ppermute | solution.py:479
  177.0 37.6 %collective-permute-start.21 = (f32[5,512,128]{2,1,0:T(8,128)}, f32[5,512,128]{2,1,0:T(8,128)}, u32[]{:S(2)}, u32[]{:S(2)}) collective-permute-start(f32[5,512,128]{2,1,0:T(8,128)} %get-tuple-element.63), channel_id=1, source_target_pairs={{1,0},{2,1},{3,2},{4,3},{5,4},{6,5},{7,6},{8,7},{9,8},{10,9},{11,1... | collective-permute-start | bytes 3932168 | tf_op jit(solution)/shard_map/ppermute | solution.py:479
  179.0 1.2 copy-start.3
  183.4 44.7 %collective-permute-start.12 = (f32[4,512,128]{2,1,0:T(8,128)}, f32[4,512,128]{2,1,0:T(8,128)S(1)}, u32[]{:S(2)}, u32[]{:S(2)}) collective-permute-start(f32[4,512,128]{2,1,0:T(8,128)} %get-tuple-element.48), channel_id=1, source_target_pairs={{0,1},{1,2},{2,3},{3,4},{4,5},{5,6},{6,7},{7,8},{8,9},{9,10},{10,1... | collective-permute-start | bytes 3145736 | tf_op jit(solution)/shard_map/ppermute | solution.py:479
  187.8 45.0 %collective-permute-start.13 = (f32[4,512,128]{2,1,0:T(8,128)}, f32[4,512,128]{2,1,0:T(8,128)S(1)}, u32[]{:S(2)}, u32[]{:S(2)}) collective-permute-start(f32[4,512,128]{2,1,0:T(8,128)} %get-tuple-element.49), channel_id=1, source_target_pairs={{1,0},{2,1},{3,2},{4,3},{5,4},{6,5},{7,6},{8,7},{9,8},{10,9},{11,1... | collective-permute-start | bytes 3145736 | tf_op jit(solution)/shard_map/ppermute | solution.py:479
  189.8 13.9 %collective-permute-start.17 = (f32[3,128,512]{2,1,0:T(8,128)}, f32[3,128,512]{2,1,0:T(8,128)}, u32[]{:S(2)}, u32[]{:S(2)}) collective-permute-start(f32[3,128,512]{2,1,0:T(8,128)} %get-tuple-element.56), channel_id=1, source_target_pairs={{16,0},{32,16},{48,32},{64,48},{80,64},{96,80},{112,96},{17,1},{33... | collective-permute-start | bytes 2359304 | tf_op jit(solution)/shard_map/ppermute | solution.py:479
  214.6 1.1 copy-start.4
  228.1 4.7 %copy-start.12 = (f32[4,512,128]{2,1,0:T(8,128)}, f32[4,512,128]{2,1,0:T(8,128)S(1)}, u32[]{:S(2)}) copy-start(f32[4,512,128]{2,1,0:T(8,128)S(1)} %collective-permute-done.12.refs_5_) | copy-start | bytes 3145732
  232.8 1.0 copy-start.13
where the time goes:
time: 242 us; the launch traced here: 240 us
  Pallas kernels  91.1 us (38%)
  starting transfers between devices  77 us (32%)
  waiting for transfers between devices  51.6 us (21%)
  local copies, waits for them, and re-layouts  11.9 us (5%)
  other arithmetic  6.14 us (3%)
    ppermute x22, starting transfers between devices, shifted(): lax.ppermute(value, axis, [(source, source + steps) for source in range(l...  77 us
    ppermute x22, waiting for transfers between devices, shifted(): lax.ppermute(value, axis, [(source, source + steps) for source in range(l...  51.6 us
    pallas_call x4, Pallas kernels, update(): pl.pallas_call(kernel, grid=(len(slices), len(columns)), in_specs=specs,...  22.4 us
    pallas_call x1, Pallas kernels, turn(): pl.pallas_call(kernel, name='turn', grid=(SLOTS,), in_specs=[SMEM, SMEM]...  21.7 us
    pallas_call x1, Pallas kernels, enter(): pl.pallas_call(kernel, name='enter', grid=(SLOTS,), in_specs=[SMEM, SMEM]...  15.6 us
    pallas_call x1, Pallas kernels, leave(): pl.pallas_call(kernel, name='leave', grid=(SLOTS,), in_specs=[SMEM, SMEM]...  11.1 us
    pallas_call x2, Pallas kernels, rims_with_rows(): pl.pallas_call(kernel, grid=(1,), in_specs=[whole] * 2 + ends * 2, out_sp...  6.94 us
    unnamed x33, local copies, waits for them, and re-layouts  6.46 us
  transfers between devices with their start and end apart: 22, of which 7 were waited for; matrix products, arithmetic and copies ran while one was open for 4% of the time, Pallas kernels for 36%

commit v1 on v0

v1 whole, which is shorter than its diff:
```python
import math

import jax
import jax.numpy as jnp
import numpy as np
from jax import lax
from jax.experimental import pallas as pl
from jax.experimental.pallas import tpu as pltpu
from jax.sharding import PartitionSpec as P


FRESNEL = 0.0005
N = 256
H = 128
SLICES = 4
SLOTS = 4
TILE = 512
F32 = jnp.float32
BF16 = jnp.bfloat16

G = 1
STEPS = SLOTS // G


def real_form(matrix):
    return np.block([[matrix.real, -matrix.imag], [matrix.imag, matrix.real]])


def split_table(pair):
    parts = np.stack([real_form(m) for m in pair]).astype(np.float32)
    high = parts.astype(BF16)
    low = (parts - high.astype(np.float32)).astype(BF16)
    return np.stack([high, low])


def tables():
    counter = np.arange(N)
    frequency = (counter + H) % N - H
    q = np.exp(1j * FRESNEL * frequency.astype(np.float64) ** 2)
    spread = np.fft.ifft(q)
    j, m = np.arange(H)[:, None], np.arange(H)[None, :]
    near, far = spread[(j - m) % N], spread[(j - m - H) % N]
    prop = ((near + far) / 2, (near - far) / 2)
    even = np.exp(-2j * np.pi * ((j * m) % H) / H) / 16
    odd = np.exp(-2j * np.pi * ((m * (2 * j + 1)) % N) / N) / 16
    prop_table, dft_table = split_table(prop), split_table((even, odd))
    return prop_table, dft_table


def fit_sincos():
    x = np.cos(np.linspace(0, np.pi, 4000)) * 3.16
    w = x * x
    fit = lambda y: [float(c) for c in np.polynomial.chebyshev.Chebyshev.fit(w, y, 3).convert(kind=np.polynomial.Polynomial).coef]
    return fit(np.sqrt(2.0) * np.sin(x / 4) / x), fit(2.0 * np.cos(x / 4))


SIN_PART, COS_PART = fit_sincos()
ROOT_2 = math.sqrt(2.0)


def poly(w, coefficients):
    total = coefficients[-1] * w + coefficients[-2]
    for c in coefficients[-3::-1]:
        total = total * w + c
    return total


def sincos(phase):
    w = phase * phase
    s, c = phase * poly(w, SIN_PART), poly(w, COS_PART)
    s2, c2 = s * c, 1.0 - s * s
    return ROOT_2 * (s2 * c2), 1.0 - s2 * s2


def split(x):
    high = x.astype(BF16)
    return high, (x - high.astype(F32)).astype(BF16)


def dot(a, b):
    return jnp.dot(a, b, preferred_element_type=F32)


def left_product(table, which, z):
    zh, zl = split(z)
    mh, ml = table[0, which], table[1, which]
    return dot(mh, zh) + dot(ml, zh) + dot(mh, zl)


def right_product(table, which, z):
    zh, zl = split(z)
    mh, ml = table[0, which], table[1, which]
    return dot(zh, mh) + dot(zh, ml) + dot(zl, mh)


def halves(x, axis):
    return (x[:H], x[H:]) if axis == 0 else (x[:, :H], x[:, H:])


def along(waves, axis, table, before, after):
    product = left_product if axis == 0 else right_product
    stacks = []
    for wave in waves:
        (r0, r1), (i0, i1) = halves(wave[0], axis), halves(wave[1], axis)
        if before:
            r0, r1, i0, i1 = r0 + r1, r0 - r1, i0 + i1, i0 - i1
        stacks.append((jnp.concatenate([r0, i0], axis), jnp.concatenate([r1, i1], axis)))
    stacks = [(product(table, 0, first), product(table, 1, second)) for first, second in stacks]
    outs = []
    for first, second in stacks:
        (r0, i0), (r1, i1) = halves(first, axis), halves(second, axis)
        if after:
            r0, r1, i0, i1 = r0 + r1, r0 - r1, i0 + i1, i0 - i1
        outs.append((jnp.concatenate([r0, r1], axis), jnp.concatenate([i0, i1], axis)))
    return outs


def both_axes(waves, left, right, before, after):
    return along(along(waves, 0, left, before, after), 1, right, before, after)


def product_of(a, b):
    return a[0] * b[0] - a[1] * b[1], a[0] * b[1] + a[1] * b[0]


def conj_product(a, b):
    return a[0] * b[0] + a[1] * b[1], a[0] * b[1] - a[1] * b[0]


class Place:
    def __init__(self, offs, count, j):
        self.used = j < count[0, 0]
        slot = jnp.where(self.used, j, 0)
        top, left = offs[0, 0, slot, 0], offs[0, 0, slot, 1]
        self.r, self.c = top & 7, left & (H - 1)
        self.row = pl.multiple_of(top - self.r, 8)
        self.wrap = pl.multiple_of(jnp.minimum(self.row + N, 3 * N - 8), 8)
        self.after = pl.multiple_of(self.row + 8, 8)
        tile = lax.shift_right_logical(left, 7)
        self.tiles = tile, tile + 1, jnp.minimum(tile + 2, 5)
        self.rows = lax.broadcasted_iota(jnp.int32, (8, H), 0) >= self.r
        self.cols = lax.broadcasted_iota(jnp.int32, (N, H), 1) >= self.c

    def column(self, tiled, plane, tile):
        first = tiled[plane, tile, pl.ds(self.row, 8), :]
        wrapped = tiled[plane, tile, pl.ds(self.wrap, 8), :]
        rest = tiled[plane, tile, pl.ds(self.after, N - 8), :]
        return jnp.concatenate([jnp.where(self.rows, first, wrapped), rest], 0)

    def take(self, tiled, plane):
        a, b, c = (self.column(tiled, plane, t) for t in self.tiles)
        return jnp.concatenate([jnp.where(self.cols, a, c), b], 1)

    def add(self, tiled, plane, value):
        first, second = value[:, :H], value[:, H:]
        parts = jnp.where(self.cols, first, 0.0), second, jnp.where(self.cols, 0.0, first)
        for tile, part in zip(self.tiles, parts):
            tiled[plane, tile, pl.ds(self.after, N - 8), :] += part[8:]
            tiled[plane, tile, pl.ds(self.row, 8), :] += jnp.where(self.rows, part[:8], 0.0)
            tiled[plane, tile, pl.ds(self.wrap, 8), :] += jnp.where(self.rows, 0.0, part[:8])

    def shifted(self, probe):
        keep = jnp.where(self.used, 1.0, 0.0)
        return tuple(pltpu.roll(pltpu.roll(probe[p], self.r, 0), self.c, 1) * keep for p in range(2))


N_COPIES = 22
QUARTERS = tuple(range(TILE // H))


def fill_pairs(padded, s, k, amp, ph, left, right, above, below, corner_a, corner_b):
    own, upper, lower = pl.ds(H, TILE), pl.ds(0, H), pl.ds(H + TILE, H)
    pairs = [(left.at[:, k], padded.at[:, 0, own, :]), (right.at[:, k], padded.at[:, 5, own, :])]
    for q in QUARTERS:
        lanes = pl.ds(q * H, H)
        pairs.append((amp.at[s, :, lanes], padded.at[0, 1 + q, own, :]))
        pairs.append((ph.at[s, :, lanes], padded.at[1, 1 + q, own, :]))
        pairs.append((above.at[:, s, :, lanes], padded.at[:, 1 + q, upper, :]))
        pairs.append((below.at[:, s, :, lanes], padded.at[:, 1 + q, lower, :]))
    for source, rows in ((corner_a, upper), (corner_b, lower)):
        pairs.append((source.at[:, k, :, pl.ds(0, H)], padded.at[:, 0, rows, :]))
        pairs.append((source.at[:, k, :, pl.ds(H, H)], padded.at[:, 5, rows, :]))
    return pairs


def copies_of(pairs, sems):
    return [pltpu.make_async_copy(a, b, sems.at[i]) for i, (a, b) in enumerate(pairs)]


def start_all(copies):
    for c in copies:
        c.start()


def wait_all(copies):
    for c in copies:
        c.wait()


def drain_pairs(totals, by_columns, centre, top, bottom, left, right):
    own, upper, lower = pl.ds(H, TILE), pl.ds(0, H), pl.ds(H + TILE, H)
    rows = pl.ds(0, 3 * N) if by_columns else own
    pairs = [(totals.at[:, 0, rows, :], left), (totals.at[:, 5, rows, :], right)]
    for q in QUARTERS:
        pairs.append((totals.at[:, 1 + q, own, :], centre.at[:, :, pl.ds(q * H, H)]))
    for q, tile in enumerate(range(1, 5) if by_columns else range(6)):
        pairs.append((totals.at[:, tile, upper, :], top.at[:, :, pl.ds(q * H, H)]))
        pairs.append((totals.at[:, tile, lower, :], bottom.at[:, :, pl.ds(q * H, H)]))
    return pairs


def fold_shapes(planes, by_columns=False):
    shape = lambda *s: jax.ShapeDtypeStruct((planes, *s), F32)
    wide, tall = (TILE, 3 * N) if by_columns else (3 * N, TILE)
    return [shape(TILE, TILE), shape(H, wide), shape(H, wide), shape(tall, H), shape(tall, H)]


ANY = pl.BlockSpec(memory_space=pl.ANY)
SMEM = pl.BlockSpec(memory_space=pltpu.SMEM)
VMEM = pl.BlockSpec(memory_space=pltpu.VMEM)
PER_SLOT = pl.BlockSpec((G, 2, N, N), lambda j: (j, 0, 0, 0))
SLOT_SHAPE = jax.ShapeDtypeStruct((SLOTS, 2, N, N), F32)
PARAMS = pltpu.CompilerParams(dimension_semantics=("arbitrary",))
TILED = lambda planes: pltpu.VMEM((planes, 6, 3 * N, H), F32)


def window_of(padded, place):
    amp, ph = place.take(padded, 0), place.take(padded, 1)
    sine, cosine = sincos(ph)
    return amp * cosine, amp * sine


def intensity(wave):
    return wave[0] * wave[0] + wave[1] * wave[1]


def waves_in(ref):
    return [(ref[g, 0], ref[g, 1]) for g in range(G)]


def put_waves(ref, waves):
    for g, wave in enumerate(waves):
        ref[g, 0], ref[g, 1] = wave


def add_all(places, totals, plane, values):
    for place, value in zip(places, values):
        place.add(totals, plane, value)


def add_grads(places, totals, plane, waves, backs):
    for place, wave, back in zip(places, waves, backs):
        real, imag = conj_product(wave, back)
        place.add(totals, plane, real)
        place.add(totals, plane + 1, imag)


def each(function, *lists):
    return [function(*items) for items in zip(*lists)]


def enter(scalars, sides, probe, prop, prop_t):
    def kernel(offs, count, *rest):
        arrays, (probe, prop, prop_t) = rest[:8], rest[8:11]
        waves, window_ref, parts = rest[11:14], rest[14], rest[15:20]
        padded, totals, sems = rest[20:]
        j = pl.program_id(0)
        fills = [copies_of(fill_pairs(padded.at[s], s, s, *arrays), sems.at[s]) for s in range(2)]
        places = lambda: [Place(offs, count, G * j + g) for g in range(G)]
        forward = lambda now, windows: both_axes(each(product_of, now, windows), prop, prop_t, True, True)

        @pl.when(j == 0)
        def _():
            start_all(fills[0])
            start_all(fills[1])
            totals[...] = jnp.zeros_like(totals)
            wait_all(fills[0])

        @pl.when(G * j < count[0, 0])
        def _():
            at = places()
            now = [place.shifted(probe) for place in at]
            put_waves(waves[0], now)
            add_all(at, totals, 0, each(intensity, now))
            now = forward(now, [window_of(padded.at[0], place) for place in at])
            put_waves(waves[1], now)
            add_all(at, totals, 1, each(intensity, now))

        @pl.when(j == 0)
        def _():
            wait_all(fills[1])

        @pl.when(G * j < count[0, 0])
        def _():
            at = places()
            windows = [window_of(padded.at[1], place) for place in at]
            put_waves(window_ref, windows)
            now = forward(waves_in(waves[1]), windows)
            put_waves(waves[2], now)
            add_all(at, totals, 2, each(intensity, now))

        @pl.when(j == STEPS - 1)
        def _():
            drains = copies_of(drain_pairs(totals, True, *parts), sems.at[0])
            start_all(drains)
            wait_all(drains)

    out = pl.pallas_call(
        kernel,
        name="enter",
        grid=(STEPS,),
        in_specs=[SMEM, SMEM] + [ANY] * 8 + [VMEM] * 3,
        out_specs=[PER_SLOT] * 4 + [ANY] * 5,
        out_shape=[SLOT_SHAPE] * 4 + fold_shapes(3, True),
        scratch_shapes=[pltpu.VMEM((2, 2, 6, 3 * N, H), F32), TILED(3), pltpu.SemaphoreType.DMA((2, N_COPIES))],
        compiler_params=PARAMS,
    )(*scalars, *sides, probe, prop, prop_t)
    return out[:3], out[3], out[4:]


def turn(scalars, sides, incident, target, prop, prop_t, dft, dft_t):
    def kernel(offs, count, *rest):
        arrays, (wave_ref, target_ref, prop, prop_t, dft, dft_t) = rest[:8], rest[8:14]
        back_ref, parts = rest[14], rest[15:20]
        padded, totals, kept_window, kept_wave, sems = rest[20:]
        j = pl.program_id(0)
        fills = [copies_of(fill_pairs(padded.at[k], k + 2, k, *arrays), sems.at[k]) for k in range(2)]
        places = lambda: [Place(offs, count, G * j + g) for g in range(G)]

        @pl.when(j == 0)
        def _():
            start_all(fills[0])
            start_all(fills[1])
            totals[...] = jnp.zeros_like(totals)
            wait_all(fills[0])

        @pl.when(G * j < count[0, 0])
        def _():
            at = places()
            windows = [window_of(padded.at[0], place) for place in at]
            put_waves(kept_window, windows)
            now = both_axes(each(product_of, waves_in(wave_ref), windows), prop, prop_t, True, True)
            put_waves(kept_wave, now)
            add_all(at, totals, 4, each(intensity, now))

        @pl.when(j == 0)
        def _():
            wait_all(fills[1])

        @pl.when(G * j < count[0, 0])
        def _():
            at = places()
            windows = [window_of(padded.at[1], place) for place in at]
            far = both_axes(each(product_of, waves_in(kept_wave), windows), dft, dft_t, True, False)
            misfits = [intensity(wave) - target_ref[g] for g, wave in enumerate(far)]
            scaled = [(misfit * wave[0], misfit * wave[1]) for misfit, wave in zip(misfits, far)]
            backs = both_axes(scaled, dft_t, dft, False, True)
            add_grads(at, totals, 0, waves_in(kept_wave), backs)
            backs = both_axes(each(conj_product, windows, backs), prop_t, prop, True, True)
            add_grads(at, totals, 2, waves_in(wave_ref), backs)
            backs = both_axes(each(conj_product, waves_in(kept_window), backs), prop_t, prop, True, True)
            put_waves(back_ref, backs)

        @pl.when(j == STEPS - 1)
        def _():
            drains = copies_of(drain_pairs(totals, True, *parts), sems.at[0])
            start_all(drains)
            wait_all(drains)

    out = pl.pallas_call(
        kernel,
        name="turn",
        grid=(STEPS,),
        in_specs=[SMEM, SMEM] + [ANY] * 8 + [PER_SLOT, pl.BlockSpec((G, N, N), lambda j: (j, 0, 0))] + [VMEM] * 4,
        out_specs=[PER_SLOT] + [ANY] * 5,
        out_shape=[SLOT_SHAPE] + fold_shapes(5, True),
        scratch_shapes=[
            pltpu.VMEM((2, 2, 6, 3 * N, H), F32),
            TILED(5),
            pltpu.VMEM((G, 2, N, N), F32),
            pltpu.VMEM((G, 2, N, N), F32),
            pltpu.SemaphoreType.DMA((2, N_COPIES)),
        ],
        compiler_params=PARAMS,
    )(*scalars, *sides, incident, target, prop, prop_t, dft, dft_t)
    return out[0], out[1:]


def leave(scalars, incident_0, incident_1, window_1, back, prop, prop_t):
    def kernel(offs, count, wave_0, wave_1, window_ref, back_ref, prop, prop_t, *rest):
        parts, (totals, sems) = rest[:5], rest[5:]
        j = pl.program_id(0)

        @pl.when(j == 0)
        def _():
            totals[...] = jnp.zeros_like(totals)

        @pl.when(G * j < count[0, 0])
        def _():
            at = [Place(offs, count, G * j + g) for g in range(G)]
            backs = waves_in(back_ref)
            add_grads(at, totals, 0, waves_in(wave_1), backs)
            backs = both_axes(each(conj_product, waves_in(window_ref), backs), prop_t, prop, True, True)
            add_grads(at, totals, 2, waves_in(wave_0), backs)

        @pl.when(j == STEPS - 1)
        def _():
            drains = copies_of(drain_pairs(totals, False, *parts), sems)
            start_all(drains)
            wait_all(drains)

    return pl.pallas_call(
        kernel,
        name="leave",
        grid=(STEPS,),
        in_specs=[SMEM, SMEM] + [PER_SLOT] * 4 + [VMEM] * 2,
        out_specs=[ANY] * 5,
        out_shape=fold_shapes(4),
        scratch_shapes=[TILED(4), pltpu.SemaphoreType.DMA((N_COPIES,))],
        compiler_params=PARAMS,
    )(*scalars, incident_0, incident_1, window_1, back, prop, prop_t)


def reorder_targets(measured):
    def kernel(m_ref, o_ref):
        r = lax.broadcasted_iota(jnp.int32, (N, N), 0)
        c = lax.broadcasted_iota(jnp.int32, (N, N), 1)

        def one_hot(to, source):
            return jnp.where(source == jnp.where(to < H, 2 * to, 2 * to - (N - 1)), 1.0, 0.0).astype(BF16)

        def thirds(x):
            a = x.astype(BF16)
            rest = x - a.astype(F32)
            b = rest.astype(BF16)
            return a, b, (rest - b.astype(F32)).astype(BF16)

        rows, cols = one_hot(r, c), one_hot(c, r)
        a, b, d = thirds(m_ref[0, 0, 0])
        x = (dot(rows, a) + dot(rows, b)) + dot(rows, d)
        a, b, d = thirds(x)
        o_ref[0] = (dot(a, cols) + dot(b, cols)) + dot(d, cols)

    return pl.pallas_call(
        kernel,
        name="reorder",
        grid=(SLOTS,),
        in_specs=[pl.BlockSpec((1, 1, 1, N, N), lambda j: (0, 0, j, 0, 0))],
        out_specs=pl.BlockSpec((1, N, N), lambda j: (j, 0, 0)),
        out_shape=jax.ShapeDtypeStruct((SLOTS, N, N), F32),
        compiler_params=PARAMS,
    )(measured)


def rims_with_rows(parts, from_above, from_below):
    left, right = parts[3:]
    planes = left.shape[0]

    def kernel(l_ref, r_ref, fal, far, fbl, fbr, lo, ro):
        for source, out, fa, fb in ((l_ref, lo, fal, fbl), (r_ref, ro, far, fbr)):
            out[:, :H, :] = source[:, :H, :] + fa[...]
            out[:, H:TILE - H, :] = source[:, H:TILE - H, :]
            out[:, TILE - H:, :] = source[:, TILE - H:, :] + fb[...]

    whole = pl.BlockSpec((planes, TILE, H), lambda i: (0, 0, 0))
    ends = [pl.BlockSpec((planes, H, H), lambda i: (0, 0, 0)), pl.BlockSpec((planes, H, H), lambda i: (0, 0, 5))]
    return pl.pallas_call(
        kernel,
        grid=(1,),
        in_specs=[whole] * 2 + ends * 2,
        out_specs=[whole] * 2,
        out_shape=[jax.ShapeDtypeStruct((planes, TILE, H), F32)] * 2,
    )(left, right, from_above, from_above, from_below, from_below)


def rims_with_columns(parts, from_left, from_right):
    top, bottom = parts[1:3]
    planes = top.shape[0]

    def kernel(t_ref, b_ref, flt, flb, frt, frb, to, bo):
        for source, out, fl, fr in ((t_ref, to, flt, frt), (b_ref, bo, flb, frb)):
            out[:, :, :H] = source[:, :, :H] + fl[...]
            out[:, :, H:TILE - H] = source[:, :, H:TILE - H]
            out[:, :, TILE - H:] = source[:, :, TILE - H:] + fr[...]

    whole = pl.BlockSpec((planes, H, TILE), lambda i: (0, 0, 0))
    ends = [pl.BlockSpec((planes, H, H), lambda i: (0, 0, 0)), pl.BlockSpec((planes, H, H), lambda i: (0, 5, 0))]
    return pl.pallas_call(
        kernel,
        grid=(1,),
        in_specs=[whole] * 2 + ends * 2,
        out_specs=[whole] * 2,
        out_shape=[jax.ShapeDtypeStruct((planes, H, TILE), F32)] * 2,
    )(top, bottom, from_left, from_left, from_right, from_right)


def shifted(value, axis, steps):
    count = lax.axis_size(axis)
    leading, last = max(0, -steps), min(count, count - steps)
    return lax.ppermute(value, axis, [(source, source + steps) for source in range(leading, last)])


def light_scale(plane, planes, centre, from_left, from_right, from_above, from_below):
    blocks = TILE // H
    at = plane // planes

    def kernel(centre, left, right, above, below, out):
        c = pl.program_id(0)
        out[...] = centre[...]
        out[:, :H, :] += above[...]
        out[:, TILE - H:, :] += below[...]

        @pl.when(c == 0)
        def _():
            out[...] += left[:, H:H + TILE, :]

        @pl.when(c == blocks - 1)
        def _():
            out[...] += right[:, H:H + TILE, :]

        out[...] = 1.0 / (out[...] + 1.0)

    column = pl.BlockSpec((planes, TILE, H), lambda c: (at, 0, c))
    side = pl.BlockSpec((planes, 3 * N, H), lambda c: (at, 0, 0))
    end = pl.BlockSpec((planes, H, H), lambda c: (at, 0, c))
    return pl.pallas_call(
        kernel,
        grid=(blocks,),
        in_specs=[column, side, side, end, end],
        out_specs=pl.BlockSpec((planes, TILE, H), lambda c: (0, 0, c)),
        out_shape=jax.ShapeDtypeStruct((planes, TILE, TILE), F32),
        compiler_params=PARAMS,
    )(centre, from_left, from_right, from_above, from_below)


OUT_SHAPE = [jax.ShapeDtypeStruct((SLICES, TILE, TILE), F32)] * 2
PARAMS_2 = pltpu.CompilerParams(dimension_semantics=("arbitrary", "arbitrary"))


def update(slices, first, amp, ph, centre, above, below, sides, scale, scale_of, previous):
    last = TILE // H - 1
    top_slice = slices[0]
    across = sides is None
    here = pl.BlockSpec((1, TILE, H), lambda a, c: (top_slice - a, 0, c))
    end = pl.BlockSpec((2, H, H), lambda a, c: (first + a, 0, c + (1 if across else 0)))
    operands = [amp, ph, centre, above, below, scale]
    specs = [here, here, pl.BlockSpec((2, TILE, H), lambda a, c: (first + a, 0, c)), end, end]
    specs.append(pl.BlockSpec((1, TILE, H), lambda a, c: (top_slice - a - scale_of, 0, c)))
    if sides:
        operands += list(sides)
        specs += [pl.BlockSpec((2, 3 * N, H), lambda a, c: (first + a, 0, 0))] * 2
    used = len(operands)
    if previous:
        operands += list(previous)
        specs += [ANY] * 2

    def kernel(*refs):
        amp_ref, ph_ref, centre, above, below, scale = refs[:6]
        out_r, out_i = refs[-2:]
        c = pl.program_id(1)

        def total(p):
            x = centre[p]
            x = jnp.concatenate([x[:H] + above[p], x[H:TILE - H], x[TILE - H:] + below[p]], 0)
            if sides:
                left, right = refs[6][p, H:H + TILE, :], refs[7][p, H:H + TILE, :]
                x = x + jnp.where(c == 0, left, jnp.where(c == last, right, 0.0))
            return x

        sine, cosine = sincos(ph_ref[0])
        out_r[0] = amp_ref[0] * cosine - total(0) * scale[0]
        out_i[0] = amp_ref[0] * sine - total(1) * scale[0]

    return pl.pallas_call(
        kernel,
        grid=(len(slices), TILE // H),
        in_specs=specs,
        out_specs=[here, here],
        out_shape=OUT_SHAPE,
        input_output_aliases={used: 0, used + 1: 1} if previous else {},
        compiler_params=PARAMS_2,
    )(*operands)


def finish(outs, sides, scale):
    def kernel(left, right, scale, in_r, in_i, out_r, out_i):
        c = pl.program_id(1)
        for p, (source, out) in enumerate(((in_r, out_r), (in_i, out_i))):
            out[0] = source[0] - jnp.where(c == 0, left[p], right[p]) * scale[0]

    here = pl.BlockSpec((1, TILE, H), lambda a, c: (1 - a, 0, 3 * c))
    side = pl.BlockSpec((2, TILE, H), lambda a, c: (a, 0, 0))
    return pl.pallas_call(
        kernel,
        name="finish",
        grid=(2, 2),
        in_specs=[side, side, here, here, here],
        out_specs=[here, here],
        out_shape=OUT_SHAPE,
        input_output_aliases={3: 0, 4: 1},
        compiler_params=PARAMS_2,
    )(*sides, scale, *outs)


def program(object_amp, object_phase, probe_field, measured, offsets, counts):
    prop, dft = lax.optimization_barrier(tuple(jnp.asarray(t) for t in tables()))
    prop_t, dft_t = jnp.swapaxes(prop, 2, 3), jnp.swapaxes(dft, 2, 3)
    amp, ph = object_amp, object_phase
    scalars = (offsets, counts)
    edges = []
    for a, b in ((0, 2), (2, 4)):
        edge = lambda cols: jnp.stack([amp[a:b, :, cols], ph[a:b, :, cols]])
        left = shifted(edge(slice(TILE - H, TILE)), "col", 1)
        right = shifted(edge(slice(0, H)), "col", -1)
        edges.append((left, right))
    above = shifted(jnp.stack([amp[:, TILE - H:], ph[:, TILE - H:]]), "row", 1)
    below = shifted(jnp.stack([amp[:, :H], ph[:, :H]]), "row", -1)
    sides = []
    for left, right in edges:
        corner = lambda rows: jnp.concatenate([left[:, :, rows], right[:, :, rows]], 3)
        corner_a = shifted(corner(slice(TILE - H, TILE)), "row", 1)
        corner_b = shifted(corner(slice(0, H)), "row", -1)
        sides.append((amp, ph, left, right, above, below, corner_a, corner_b))
    target = reorder_targets(measured)

    waves, window_1, lights = enter(scalars, sides[0], probe_field, prop, prop_t)
    light_left = shifted(lights[4], "col", 1)
    light_right = shifted(lights[3], "col", -1)

    back, grads_a = turn(scalars, sides[1], waves[2], target, prop, prop_t, dft, dft_t)
    a_left = shifted(grads_a[4], "col", 1)
    a_right = shifted(grads_a[3], "col", -1)

    grads_b = leave(scalars, waves[0], waves[1], window_1, back, prop, prop_t)
    b_above = shifted(grads_b[2], "row", 1)
    b_below = shifted(grads_b[1], "row", -1)

    to_up, to_down = rims_with_columns(lights, light_left, light_right)
    light_above = shifted(to_down, "row", 1)
    light_below = shifted(to_up, "row", -1)
    scale = light_scale(0, 3, lights[0], light_left, light_right, light_above, light_below)

    to_left, to_right = rims_with_rows(grads_b, b_above, b_below)
    b_sides = shifted(to_right, "col", 1), shifted(to_left, "col", -1)

    to_up, to_down = rims_with_columns(grads_a, a_left, a_right)
    a_above = shifted(to_down, "row", 1)
    a_below = shifted(to_up, "row", -1)
    scale_3 = light_scale(4, 1, grads_a[0], a_left, a_right, a_above, a_below)

    a_parts = (grads_a[0], a_above, a_below, (a_left, a_right))
    outs = update((1, 0), 0, amp, ph, grads_b[0], b_above, b_below, None, scale, 0, None)
    outs = update((3,), 0, amp, ph, *a_parts, scale_3, 3, outs)
    outs = update((2,), 1, amp, ph, *a_parts, scale, 0, outs)
    return tuple(finish(outs, b_sides, scale))


def solution(mesh):
    placed = (
        P(None, "row", "col"),
        P(None, "row", "col"),
        P(),
        P("row", "col", None, None, None),
        P("row", "col", None, None),
        P("row", "col"),
    )
    return jax.shard_map(
        program,
        mesh=mesh,
        in_specs=placed,
        out_specs=(P(None, "row", "col"), P(None, "row", "col")),
        check_vma=False,
    )
```

time: 242 us -> 279 us (1.15)
  waiting for transfers between devices: 51.6 us -> 86.1 us
  Pallas kernels: 91.1 us -> 94.6 us
    ppermute x22, waiting for transfers between devices: 51.6 us -> 86.1 us  [shifted(): lax.ppermute(value, axis, [(source, source + steps) for source in range(l...]
    pallas_call x9 -> x11, Pallas kernels: 79.5 us -> 86.7 us  [the longest x1 20.6 us: turn(): pl.pallas_call(kernel, name='turn', grid=(STEPS,), in_specs=[SMEM, SMEM]...]
    pallas_call x2 -> x1, Pallas kernels: 6.94 us -> 3.24 us  [rims_with_rows(): pl.pallas_call(kernel, grid=(1,), in_specs=[whole] * 2 + ends * 2, out_sp...]
  transfers between devices with their start and end apart: 22 -> 22, of which waited for: 7 -> 5; matrix products, arithmetic and copies ran while one was open for 4% -> 3% of each run, Pallas kernels for 36% -> 33%
where the time goes in v1:
time: 279 us; the launch traced here: 276 us
  Pallas kernels  94.6 us (34%)
  waiting for transfers between devices  86.1 us (31%)
  starting transfers between devices  75.3 us (27%)
  local copies, waits for them, and re-layouts  12.3 us (4%)
  other arithmetic  6.14 us (2%)
    ppermute x22, waiting for transfers between devices, shifted(): lax.ppermute(value, axis, [(source, source + steps) for source in range(l...  86.1 us
    ppermute x22, starting transfers between devices, shifted(): lax.ppermute(value, axis, [(source, source + steps) for source in range(l...  75.3 us
    pallas_call x1, Pallas kernels, turn(): pl.pallas_call(kernel, name='turn', grid=(STEPS,), in_specs=[SMEM, SMEM]...  20.6 us
    pallas_call x3, Pallas kernels, update(): pl.pallas_call(kernel, grid=(len(slices), TILE // H), in_specs=specs, out...  20.2 us
    pallas_call x1, Pallas kernels, enter(): pl.pallas_call(kernel, name='enter', grid=(STEPS,), in_specs=[SMEM, SMEM]...  14.5 us
    pallas_call x1, Pallas kernels, leave(): pl.pallas_call(kernel, name='leave', grid=(STEPS,), in_specs=[SMEM, SMEM]...  10.4 us
    pallas_call x2, Pallas kernels, light_scale(): pl.pallas_call(kernel, grid=(blocks,), in_specs=[column, side, side, end,...  9.86 us
    unnamed x33, local copies, waits for them, and re-layouts  6.82 us
  transfers between devices with their start and end apart: 22, of which 5 were waited for; matrix products, arithmetic and copies ran while one was open for 3% of the time, Pallas kernels for 33%

profile of v1, /device:TPU:49, one launch (start us, length us, event | category | flops | bytes accessed | tf_op | source)
XLA Modules:
  0.0 276.1 jit_solution(3328498825558823488)
XLA Ops:
  0.6 2.7 slice_bitcast_fusion.4
  3.4 3.8 %collective-permute-start = (f32[2,2,512,128]{3,2,1,0:T(8,128)S(1)}, f32[2,2,512,128]{3,2,1,0:T(8,128)S(1)}, u32[]{:S(2)}, u32[]{:S(2)}) collective-permute-start(f32[2,2,512,128]{3,2,1,0:T(8,128)S(1)} %pad_maximum_fusion.2), channel_id=1, source_target_pairs={{0,1},{1,2},{2,3},{3,4},{4,5},{5,6},{6,7},{7,8},{8,9},{9,10},{10,1... | collective-permute-start | bytes 3145736 | tf_op jit(solution)/shard_map/ppermute | solution.py:500
  7.3 1.9 collective-permute-start.1
  9.8 1.6 pad_maximum_fusion
  11.5 3.9 %collective-permute-start.2 = (f32[2,4,128,512]{3,2,1,0:T(8,128)}, f32[2,4,128,512]{3,2,1,0:T(8,128)S(1)}, u32[]{:S(2)}, u32[]{:S(2)}) collective-permute-start(f32[2,4,128,512]{3,2,1,0:T(8,128)} %pad_maximum_fusion), channel_id=1, source_target_pairs={{0,16},{16,32},{32,48},{48,64},{64,80},{80,96},{96,112},{1,17},{17... | collective-permute-start | bytes 6291464 | tf_op jit(solution)/shard_map/ppermute | solution.py:500
  15.4 1.6 pad_maximum_fusion.1
  17.0 1.9 collective-permute-start.3
  19.0 3.5 %collective-permute-start.6 = (f32[2,2,512,128]{3,2,1,0:T(8,128)S(1)}, f32[2,2,512,128]{3,2,1,0:T(8,128)S(1)}, u32[]{:S(2)}, u32[]{:S(2)}) collective-permute-start(f32[2,2,512,128]{3,2,1,0:T(8,128)S(1)} %pad_maximum_fusion.4), channel_id=1, source_target_pairs={{0,1},{1,2},{2,3},{3,4},{4,5},{5,6},{6,7},{7,8},{8,9},{9,10},{10,1... | collective-permute-start | bytes 3145736 | tf_op jit(solution)/shard_map/ppermute | solution.py:500
  22.6 7.0 %collective-permute-done.rest_2_ = f32[2,2,512,128]{3,2,1,0:T(8,128)S(1)} collective-permute-done((f32[2,2,512,128]{3,2,1,0:T(8,128)S(1)}, f32[2,2,512,128]{3,2,1,0:T(8,128)S(1)}, u32[]{:S(2)}, u32[]{:S(2)}) %collective-permute-start) | collective-permute-done | bytes 1048608 | tf_op jit(solution)/shard_map/ppermute | solution.py:500
  29.6 1.9 collective-permute-start.7
  33.0 4.7 %collective-permute-start.4 = (f32[2,2,128,256]{3,2,1,0:T(8,128)S(1)}, f32[2,2,128,256]{3,2,1,0:T(8,128)S(1)}, u32[]{:S(2)}, u32[]{:S(2)}) collective-permute-start(f32[2,2,128,256]{3,2,1,0:T(8,128)S(1)} %pad_maximum_fusion.6), channel_id=1, source_target_pairs={{0,16},{16,32},{32,48},{48,64},{64,80},{80,96},{96,112},{1,17},{17... | collective-permute-start | bytes 1572872 | tf_op jit(solution)/shard_map/ppermute | solution.py:500
  38.6 13.4 %collective-permute-done.6.rest_2_ = f32[2,2,512,128]{3,2,1,0:T(8,128)S(1)} collective-permute-done((f32[2,2,512,128]{3,2,1,0:T(8,128)S(1)}, f32[2,2,512,128]{3,2,1,0:T(8,128)S(1)}, u32[]{:S(2)}, u32[]{:S(2)}) %collective-permute-start.6) | collective-permute-done | bytes 1048608 | tf_op jit(solution)/shard_map/ppermute | solution.py:500
  52.1 3.4 %collective-permute-start.5 = (f32[2,2,128,256]{3,2,1,0:T(8,128)}, f32[2,2,128,256]{3,2,1,0:T(8,128)}, u32[]{:S(2)}, u32[]{:S(2)}) collective-permute-start(f32[2,2,128,256]{3,2,1,0:T(8,128)} %pad_maximum_fusion.7), channel_id=1, source_target_pairs={{16,0},{32,16},{48,32},{64,48},{80,64},{96,80},{112,96},{17,1},{33... | collective-permute-start | bytes 1572872 | tf_op jit(solution)/shard_map/ppermute | solution.py:500
  56.6 4.4 %collective-permute-start.8 = (f32[2,2,128,256]{3,2,1,0:T(8,128)}, f32[2,2,128,256]{3,2,1,0:T(8,128)}, u32[]{:S(2)}, u32[]{:S(2)}) collective-permute-start(f32[2,2,128,256]{3,2,1,0:T(8,128)} %pad_maximum_fusion.8), channel_id=1, source_target_pairs={{0,16},{16,32},{32,48},{48,64},{64,80},{80,96},{96,112},{1,17},{17... | collective-permute-start | bytes 1572872 | tf_op jit(solution)/shard_map/ppermute | solution.py:500
  61.8 1.9 collective-permute-start.9
  64.5 1.0 copy.17.rest_9_.rest_10_.prop
  65.5 1.3 copy-done.5
  66.8 14.5 %enter.1 = (f32[4,2,256,256]{3,2,1,0:T(8,128)}, f32[4,2,256,256]{3,2,1,0:T(8,128)}, f32[4,2,256,256]{3,2,1,0:T(8,128)}, f32[4,2,256,256]{3,2,1,0:T(8,128)}, f32[...) custom-call(s32[1,1,4,2]{3,2,1,0:T(4,128)} %copy.21.offs, ...), custom_call_target="tpu_custom_call" | custom-call | tf_op jit(solution)/shard_map/enter/pallas_call | solution.py:308
  81.4 6.8 %collective-permute-start.14 = (f32[3,768,128]{2,1,0:T(8,128)}, f32[3,768,128]{2,1,0:T(8,128)}, u32[]{:S(2)}, u32[]{:S(2)}) collective-permute-start(f32[3,768,128]{2,1,0:T(8,128)} %get-tuple-element.50), channel_id=1, source_target_pairs={{0,1},{1,2},{2,3},{3,4},{4,5},{5,6},{6,7},{7,8},{8,9},{9,10},{10,1... | collective-permute-start | bytes 3538952 | tf_op jit(solution)/shard_map/ppermute | solution.py:500
  88.2 1.0 copy.20.rest_12_
  89.3 4.6 %reorder.1.rest_9_ = f32[4,256,256]{2,1,0:T(8,128)} custom-call(f32[1,1,4,256,256]{4,3,2,1,0:T(8,128)} %m_ref.1), custom_call_target="tpu_custom_call" | custom-call | tf_op jit(solution)/shard_map/reorder/pallas_call | solution.py:444
  93.9 20.6 %turn.1 = (f32[4,2,256,256]{3,2,1,0:T(8,128)}, f32[5,512,512]{2,1,0:T(8,128)}, f32[5,128,512]{2,1,0:T(8,128)}, f32[5,128,512]{2,1,0:T(8,128)}, f32[5,768,128]{2,1,0:T(8,128)}, /*index=5*/f32[5,768,128]{2,1,0:T(8,128)}) custom-call(s32[1,1,4,2]{3,2,1,0:T(4,128)} %copy.21.offs, s32[1,1]{1,0:T(1,128)S(6)} %copy.29.count, f32[4,512,512]{2,1,0:T(8,128)} %refs_0_.5, ...), custom_call_target="tpu_custom_call" | custom-call | tf_op jit(solution)/shard_map/turn/pallas_call | solution.py:370
  114.5 12.9 %collective-permute-start.18 = (f32[5,768,128]{2,1,0:T(8,128)}, f32[5,768,128]{2,1,0:T(8,128)S(1)}, u32[]{:S(2)}, u32[]{:S(2)}) collective-permute-start(f32[5,768,128]{2,1,0:T(8,128)} %get-tuple-element.59), channel_id=1, source_target_pairs={{0,1},{1,2},{2,3},{3,4},{4,5},{5,6},{6,7},{7,8},{8,9},{9,10},{10,1... | collective-permute-start | bytes 5898248 | tf_op jit(solution)/shard_map/ppermute | solution.py:500
  127.4 1.9 collective-permute-start.19
  129.3 2.1 collective-permute-start.15
  131.4 10.4 %leave.1 = (f32[4,512,512]{2,1,0:T(8,128)}, f32[4,128,768]{2,1,0:T(8,128)}, f32[4,128,768]{2,1,0:T(8,128)}, f32[4,512,128]{2,1,0:T(8,128)}, f32[4,512,128]{2,1,0:T(8,128)}) custom-call(s32[1,1,4,2]{3,2,1,0:T(4,128)} %copy.21.offs, s32[1,1]{1,0:T(1,128)S(6)} %copy.29.count, f32[4,2,256,256]{3,2,1,0:T(8,128)} %get-tuple-element.37.wave_0, ...), custom_call_target="tpu_custom_call" | custom-call | tf_op jit(solution)/shard_map/leave/pallas_call | solution.py:412
  141.8 1.9 collective-permute-start.10
  143.8 2.4 collective-permute-start.11
  146.2 53.3 %collective-permute-done.15.frt.frb.right = f32[3,768,128]{2,1,0:T(8,128)} collective-permute-done((f32[3,768,128]{2,1,0:T(8,128)}, f32[3,768,128]{2,1,0:T(8,128)}, u32[]{:S(2)}, u32[]{:S(2)}) %collective-permute-start.15) | collective-permute-done | bytes 1179680 | tf_op jit(solution)/shard_map/ppermute | solution.py:500
  199.5 2.8 %shard_map.96 = (f32[3,128,512]{2,1,0:T(8,128)}, f32[3,128,512]{2,1,0:T(8,128)}) custom-call(f32[3,128,512]{2,1,0:T(8,128)} %get-tuple-element.52.t_ref, f32[3,128,512]{2,1,0:T(8,128)} %get-tuple-element.53.b_ref, f32[3,768,128]{2,1,0:T(8,128)} %collective-permute-done.14.flt.flb.left, f32[3,768,128]{2,1,0:T(8,128)} %collective-permute-done.14.flt.flb.left, ...), custom_call_target="tpu_custom_call" | custom-call | tf_op jit(solution)/shard_map/pallas_call | solution.py:488
  202.3 1.9 collective-permute-start.16
  204.3 1.2 copy-done.2
  205.5 3.7 %shard_map.98 = (f32[5,128,512]{2,1,0:T(8,128)}, f32[5,128,512]{2,1,0:T(8,128)}) custom-call(f32[5,128,512]{2,1,0:T(8,128)} %get-tuple-element.57.t_ref, f32[5,128,512]{2,1,0:T(8,128)} %get-tuple-element.58.b_ref, f32[5,768,128]{2,1,0:T(8,128)} %copy-done.2, f32[5,768,128]{2,1,0:T(8,128)} %copy-done.2, ...), custom_call_target="tpu_custom_call" | custom-call | tf_op jit(solution)/shard_map/pallas_call | solution.py:488
  209.3 1.9 collective-permute-start.20
  211.2 2.4 collective-permute-start.21
  213.6 1.2 copy-done.3
  214.8 3.2 %shard_map.95 = (f32[4,512,128]{2,1,0:T(8,128)}, f32[4,512,128]{2,1,0:T(8,128)}) custom-call(f32[4,512,128]{2,1,0:T(8,128)} %get-tuple-element.43.l_ref, f32[4,512,128]{2,1,0:T(8,128)} %get-tuple-element.44.r_ref, f32[4,128,768]{2,1,0:T(8,128)} %copy-done.3, f32[4,128,768]{2,1,0:T(8,128)} %copy-done.3, ...), custom_call_target="tpu_custom_call" | custom-call | tf_op jit(solution)/shard_map/pallas_call | solution.py:467
  218.0 2.0 collective-permute-start.12
  220.1 3.3 %collective-permute-start.13 = (f32[4,512,128]{2,1,0:T(8,128)}, f32[4,512,128]{2,1,0:T(8,128)S(1)}, u32[]{:S(2)}, u32[]{:S(2)}) collective-permute-start(f32[4,512,128]{2,1,0:T(8,128)} %get-tuple-element.48), channel_id=1, source_target_pairs={{1,0},{2,1},{3,2},{4,3},{5,4},{6,5},{7,6},{8,7},{9,8},{10,9},{11,1... | collective-permute-start | bytes 3145736 | tf_op jit(solution)/shard_map/ppermute | solution.py:500
  223.4 4.2 %collective-permute-start.17 = (f32[3,128,512]{2,1,0:T(8,128)}, f32[3,128,512]{2,1,0:T(8,128)}, u32[]{:S(2)}, u32[]{:S(2)}) collective-permute-start(f32[3,128,512]{2,1,0:T(8,128)} %get-tuple-element.55), channel_id=1, source_target_pairs={{16,0},{32,16},{48,32},{64,48},{80,64},{96,80},{112,96},{17,1},{33... | collective-permute-start | bytes 2359304 | tf_op jit(solution)/shard_map/ppermute | solution.py:500
  227.6 11.4 %collective-permute-done.17.below = f32[3,128,512]{2,1,0:T(8,128)} collective-permute-done((f32[3,128,512]{2,1,0:T(8,128)}, f32[3,128,512]{2,1,0:T(8,128)}, u32[]{:S(2)}, u32[]{:S(2)}) %collective-permute-start.17) | collective-permute-done | bytes 786464 | tf_op jit(solution)/shard_map/ppermute | solution.py:500
  239.0 5.9 %shard_map.97.refs_5_.scale = f32[3,512,512]{2,1,0:T(8,128)} custom-call(f32[3,512,512]{2,1,0:T(8,128)} %get-tuple-element.49.centre, f32[3,768,128]{2,1,0:T(8,128)} %collective-permute-done.14.flt.flb.left, f32[3,768,128]{2,1,0:T(8,128)} %collective-permute-done.15.frt.frb.right, f32[3,128,512]{2,1,0:T(8,128)} %collective-permute-done.16.above, ...), custom_call_target="tpu_custom_call" | custom-call | tf_op jit(solution)/shard_map/pallas_call | solution.py:526
  244.9 8.9 %shard_map.100 = (f32[4,512,512]{2,1,0:T(8,128)}, f32[4,512,512]{2,1,0:T(8,128)}) custom-call(f32[4,512,512]{2,1,0:T(8,128)} %refs_0_.5, f32[4,512,512]{2,1,0:T(8,128)} %refs_1_.5, f32[4,512,512]{2,1,0:T(8,128)} %get-tuple-element.63.refs_2_, f32[4,128,768]{2,1,0:T(8,128)} %copy-done.3, f32[4,128,768]{2,1,0:T(8,128)} %collective-permute-done.11.fbl.fbr.refs_4_, ...), custom_call_target="tpu_custom_call" | custom-call | tf_op jit(solution)/shard_map/pallas_call | solution.py:574
  253.8 1.1 copy-done.4
  254.9 4.0 %shard_map.99.refs_5_ = f32[1,512,512]{2,1,0:T(8,128)} custom-call(f32[5,512,512]{2,1,0:T(8,128)} %get-tuple-element.56.centre.refs_2_, f32[5,768,128]{2,1,0:T(8,128)} %copy-done.2, f32[5,768,128]{2,1,0:T(8,128)} %collective-permute-done.19.frt.frb.right.refs_7_, f32[5,128,512]{2,1,0:T(8,128)} %copy-done.4, f32[5,128,512]{2,1,0:T(8,128)} %collective-permute-done.21.below.refs_4_), custom_call_target="tpu_custom_call" | custom-call | tf_op jit(solution)/shard_map/pallas_call | solution.py:526
  258.9 5.7 %shard_map.101 = (f32[4,512,512]{2,1,0:T(8,128)}, f32[4,512,512]{2,1,0:T(8,128)}) custom-call(f32[4,512,512]{2,1,0:T(8,128)} %refs_0_.5, f32[4,512,512]{2,1,0:T(8,128)} %refs_1_.5, f32[5,512,512]{2,1,0:T(8,128)} %get-tuple-element.56.centre.refs_2_, f32[5,128,512]{2,1,0:T(8,128)} %copy-done.4, ...), custom_call_target="tpu_custom_call", output_to_operand_aliasing={{0}: (8, {}), {1}: (9, {})} | custom-call | tf_op jit(solution)/shard_map/pallas_call | solution.py:574
  264.6 5.6 %shard_map.102 = (f32[4,512,512]{2,1,0:T(8,128)}, f32[4,512,512]{2,1,0:T(8,128)}) custom-call(f32[4,512,512]{2,1,0:T(8,128)} %refs_0_.5, f32[4,512,512]{2,1,0:T(8,128)} %refs_1_.5, f32[5,512,512]{2,1,0:T(8,128)} %get-tuple-element.56.centre.refs_2_, f32[5,128,512]{2,1,0:T(8,128)} %copy-done.4, ...), custom_call_target="tpu_custom_call", output_to_operand_aliasing={{0}: (8, {}), {1}: (9, {})} | custom-call | tf_op jit(solution)/shard_map/pallas_call | solution.py:574
  271.6 4.6 %finish.1 = (f32[4,512,512]{2,1,0:T(8,128)}, f32[4,512,512]{2,1,0:T(8,128)}) custom-call(f32[4,512,128]{2,1,0:T(8,128)} %copy-done.12, f32[4,512,128]{2,1,0:T(8,128)} %copy-done.13, f32[3,512,512]{2,1,0:T(8,128)} %shard_map.97.refs_5_.scale, f32[4,512,512]{2,1,0:T(8,128)} %get-tuple-element.68.in_r, ...), custom_call_target="tpu_custom_call", output_to_operand_aliasing={{0}: (3, {}), {1}: (4, {})} | custom-call | tf_op jit(solution)/shard_map/finish/pallas_call | solution.py:593
  (60 shorter events, 6.5 us)
Async XLA Ops:
  0.6 8.6 %copy-start.1 = (f32[4,512,512]{2,1,0:T(8,128)S(1)}, f32[4,512,512]{2,1,0:T(8,128)}, u32[]{:S(2)}) copy-start(f32[4,512,512]{2,1,0:T(8,128)} %refs_1_.5) | copy-start | bytes 12582916
  3.3 5.9 %copy-start = (f32[4,512,512]{2,1,0:T(8,128)S(1)}, f32[4,512,512]{2,1,0:T(8,128)}, u32[]{:S(2)}) copy-start(f32[4,512,512]{2,1,0:T(8,128)} %refs_0_.5) | copy-start | bytes 12582916
  3.4 26.2 %collective-permute-start = (f32[2,2,512,128]{3,2,1,0:T(8,128)S(1)}, f32[2,2,512,128]{3,2,1,0:T(8,128)S(1)}, u32[]{:S(2)}, u32[]{:S(2)}) collective-permute-start(f32[2,2,512,128]{3,2,1,0:T(8,128)S(1)} %pad_maximum_fusion.2), channel_id=1, source_target_pairs={{0,1},{1,2},{2,3},{3,4},{4,5},{5,6},{6,7},{7,8},{8,9},{9,10},{10,1... | collective-permute-start | bytes 3145736 | tf_op jit(solution)/shard_map/ppermute | solution.py:500
  7.3 25.7 %collective-permute-start.1 = (f32[2,2,512,128]{3,2,1,0:T(8,128)S(1)}, f32[2,2,512,128]{3,2,1,0:T(8,128)S(1)}, u32[]{:S(2)}, u32[]{:S(2)}) collective-permute-start(f32[2,2,512,128]{3,2,1,0:T(8,128)S(1)} %pad_maximum_fusion.3), channel_id=1, source_target_pairs={{1,0},{2,1},{3,2},{4,3},{5,4},{6,5},{7,6},{8,7},{9,8},{10,9},{11,1... | collective-permute-start | bytes 3145736 | tf_op jit(solution)/shard_map/ppermute | solution.py:500
  11.5 54.1 %collective-permute-start.2 = (f32[2,4,128,512]{3,2,1,0:T(8,128)}, f32[2,4,128,512]{3,2,1,0:T(8,128)S(1)}, u32[]{:S(2)}, u32[]{:S(2)}) collective-permute-start(f32[2,4,128,512]{3,2,1,0:T(8,128)} %pad_maximum_fusion), channel_id=1, source_target_pairs={{0,16},{16,32},{32,48},{48,64},{64,80},{80,96},{96,112},{1,17},{17... | collective-permute-start | bytes 6291464 | tf_op jit(solution)/shard_map/ppermute | solution.py:500
  17.0 48.5 %collective-permute-start.3 = (f32[2,4,128,512]{3,2,1,0:T(8,128)}, f32[2,4,128,512]{3,2,1,0:T(8,128)}, u32[]{:S(2)}, u32[]{:S(2)}) collective-permute-start(f32[2,4,128,512]{3,2,1,0:T(8,128)} %pad_maximum_fusion.1), channel_id=1, source_target_pairs={{16,0},{32,16},{48,32},{64,48},{80,64},{96,80},{112,96},{17,1},{33... | collective-permute-start | bytes 6291464 | tf_op jit(solution)/shard_map/ppermute | solution.py:500
  19.0 33.1 %collective-permute-start.6 = (f32[2,2,512,128]{3,2,1,0:T(8,128)S(1)}, f32[2,2,512,128]{3,2,1,0:T(8,128)S(1)}, u32[]{:S(2)}, u32[]{:S(2)}) collective-permute-start(f32[2,2,512,128]{3,2,1,0:T(8,128)S(1)} %pad_maximum_fusion.4), channel_id=1, source_target_pairs={{0,1},{1,2},{2,3},{3,4},{4,5},{5,6},{6,7},{7,8},{8,9},{9,10},{10,1... | collective-permute-start | bytes 3145736 | tf_op jit(solution)/shard_map/ppermute | solution.py:500
  29.6 9.0 %copy-start.9 = (f32[2,2,512,128]{3,2,1,0:T(8,128)}, f32[2,2,512,128]{3,2,1,0:T(8,128)S(1)}, u32[]{:S(2)}) copy-start(f32[2,2,512,128]{3,2,1,0:T(8,128)S(1)} %collective-permute-done.rest_2_) | copy-start | bytes 3145732
  29.6 26.0 %collective-permute-start.7 = (f32[2,2,512,128]{3,2,1,0:T(8,128)S(1)}, f32[2,2,512,128]{3,2,1,0:T(8,128)S(1)}, u32[]{:S(2)}, u32[]{:S(2)}) collective-permute-start(f32[2,2,512,128]{3,2,1,0:T(8,128)S(1)} %pad_maximum_fusion.5), channel_id=1, source_target_pairs={{1,0},{2,1},{3,2},{4,3},{5,4},{6,5},{7,6},{8,7},{9,8},{10,9},{11,1... | collective-permute-start | bytes 3145736 | tf_op jit(solution)/shard_map/ppermute | solution.py:500
  33.0 22.6 %copy-start.10 = (f32[2,2,512,128]{3,2,1,0:T(8,128)}, f32[2,2,512,128]{3,2,1,0:T(8,128)S(1)}, u32[]{:S(2)}) copy-start(f32[2,2,512,128]{3,2,1,0:T(8,128)S(1)} %collective-permute-done.1.rest_3_) | copy-start | bytes 3145732
  33.0 28.8 %collective-permute-start.4 = (f32[2,2,128,256]{3,2,1,0:T(8,128)S(1)}, f32[2,2,128,256]{3,2,1,0:T(8,128)S(1)}, u32[]{:S(2)}, u32[]{:S(2)}) collective-permute-start(f32[2,2,128,256]{3,2,1,0:T(8,128)S(1)} %pad_maximum_fusion.6), channel_id=1, source_target_pairs={{0,16},{16,32},{32,48},{48,64},{64,80},{80,96},{96,112},{1,17},{17... | collective-permute-start | bytes 1572872 | tf_op jit(solution)/shard_map/ppermute | solution.py:500
  38.6 25.2 %copy-start.15 = (s32[1,1,4,2]{2,3,1,0:T(2,128)S(1)}, s32[1,1,4,2]{2,3,1,0:T(2,128)}, u32[]{:S(2)}) copy-start(s32[1,1,4,2]{2,3,1,0:T(2,128)} %param.12) | copy-start | bytes 100
  38.6 25.9 %copy-start.6 = (bf16[2,2,256,256]{2,3,1,0:T(8,128)(2,1)S(1)}, bf16[2,2,256,256]{2,3,1,0:T(8,128)(2,1)}, u32[]{:S(2)}) copy-start(bf16[2,2,256,256]{2,3,1,0:T(8,128)(2,1)} %constant.4.clone) | copy-start | bytes 1572868
  52.1 9.8 %copy-start.7 = (f32[2,2,512,128]{3,2,1,0:T(8,128)}, f32[2,2,512,128]{3,2,1,0:T(8,128)S(1)}, u32[]{:S(2)}) copy-start(f32[2,2,512,128]{3,2,1,0:T(8,128)S(1)} %collective-permute-done.6.rest_2_) | copy-start | bytes 3145732
  52.1 13.4 %collective-permute-start.5 = (f32[2,2,128,256]{3,2,1,0:T(8,128)}, f32[2,2,128,256]{3,2,1,0:T(8,128)}, u32[]{:S(2)}, u32[]{:S(2)}) collective-permute-start(f32[2,2,128,256]{3,2,1,0:T(8,128)} %pad_maximum_fusion.7), channel_id=1, source_target_pairs={{16,0},{32,16},{48,32},{64,48},{80,64},{96,80},{112,96},{17,1},{33... | collective-permute-start | bytes 1572872 | tf_op jit(solution)/shard_map/ppermute | solution.py:500
  55.6 6.3 %copy-start.8 = (f32[2,2,512,128]{3,2,1,0:T(8,128)}, f32[2,2,512,128]{3,2,1,0:T(8,128)S(1)}, u32[]{:S(2)}) copy-start(f32[2,2,512,128]{3,2,1,0:T(8,128)S(1)} %collective-permute-done.7.rest_3_) | copy-start | bytes 3145732
  56.6 37.3 %collective-permute-start.8 = (f32[2,2,128,256]{3,2,1,0:T(8,128)}, f32[2,2,128,256]{3,2,1,0:T(8,128)}, u32[]{:S(2)}, u32[]{:S(2)}) collective-permute-start(f32[2,2,128,256]{3,2,1,0:T(8,128)} %pad_maximum_fusion.8), channel_id=1, source_target_pairs={{0,16},{16,32},{32,48},{48,64},{64,80},{80,96},{96,112},{1,17},{17... | collective-permute-start | bytes 1572872 | tf_op jit(solution)/shard_map/ppermute | solution.py:500
  61.8 3.7 %copy-start.14 = (f32[2,2,128,256]{3,2,1,0:T(8,128)}, f32[2,2,128,256]{3,2,1,0:T(8,128)S(1)}, u32[]{:S(2)}) copy-start(f32[2,2,128,256]{3,2,1,0:T(8,128)S(1)} %collective-permute-done.4.rest_6_) | copy-start | bytes 1572868
  61.8 32.0 %collective-permute-start.9 = (f32[2,2,128,256]{3,2,1,0:T(8,128)}, f32[2,2,128,256]{3,2,1,0:T(8,128)}, u32[]{:S(2)}, u32[]{:S(2)}) collective-permute-start(f32[2,2,128,256]{3,2,1,0:T(8,128)} %pad_maximum_fusion.9), channel_id=1, source_target_pairs={{16,0},{32,16},{48,32},{64,48},{80,64},{96,80},{112,96},{17,1},{33... | collective-permute-start | bytes 1572872 | tf_op jit(solution)/shard_map/ppermute | solution.py:500
  65.5 1.3 copy-start.5
  66.8 21.4 %copy-start.11 = (bf16[2,2,256,256]{2,3,1,0:T(8,128)(2,1)S(1)}, bf16[2,2,256,256]{2,3,1,0:T(8,128)(2,1)}, u32[]{:S(2)}) copy-start(bf16[2,2,256,256]{2,3,1,0:T(8,128)(2,1)} %constant.5.clone) | copy-start | bytes 1572868
  81.4 62.4 %collective-permute-start.14 = (f32[3,768,128]{2,1,0:T(8,128)}, f32[3,768,128]{2,1,0:T(8,128)}, u32[]{:S(2)}, u32[]{:S(2)}) collective-permute-start(f32[3,768,128]{2,1,0:T(8,128)} %get-tuple-element.50), channel_id=1, source_target_pairs={{0,1},{1,2},{2,3},{3,4},{4,5},{5,6},{6,7},{7,8},{8,9},{9,10},{10,1... | collective-permute-start | bytes 3538952 | tf_op jit(solution)/shard_map/ppermute | solution.py:500
  114.5 89.8 %collective-permute-start.18 = (f32[5,768,128]{2,1,0:T(8,128)}, f32[5,768,128]{2,1,0:T(8,128)S(1)}, u32[]{:S(2)}, u32[]{:S(2)}) collective-permute-start(f32[5,768,128]{2,1,0:T(8,128)} %get-tuple-element.59), channel_id=1, source_target_pairs={{0,1},{1,2},{2,3},{3,4},{4,5},{5,6},{6,7},{7,8},{8,9},{9,10},{10,1... | collective-permute-start | bytes 5898248 | tf_op jit(solution)/shard_map/ppermute | solution.py:500
  127.4 76.9 %collective-permute-start.19 = (f32[5,768,128]{2,1,0:T(8,128)}, f32[5,768,128]{2,1,0:T(8,128)}, u32[]{:S(2)}, u32[]{:S(2)}) collective-permute-start(f32[5,768,128]{2,1,0:T(8,128)} %get-tuple-element.60), channel_id=1, source_target_pairs={{1,0},{2,1},{3,2},{4,3},{5,4},{6,5},{7,6},{8,7},{9,8},{10,9},{11,1... | collective-permute-start | bytes 5898248 | tf_op jit(solution)/shard_map/ppermute | solution.py:500
  129.3 70.2 %collective-permute-start.15 = (f32[3,768,128]{2,1,0:T(8,128)}, f32[3,768,128]{2,1,0:T(8,128)}, u32[]{:S(2)}, u32[]{:S(2)}) collective-permute-start(f32[3,768,128]{2,1,0:T(8,128)} %get-tuple-element.51), channel_id=1, source_target_pairs={{1,0},{2,1},{3,2},{4,3},{5,4},{6,5},{7,6},{8,7},{9,8},{10,9},{11,1... | collective-permute-start | bytes 3538952 | tf_op jit(solution)/shard_map/ppermute | solution.py:500
  141.8 71.7 %collective-permute-start.10 = (f32[4,128,768]{2,1,0:T(8,128)}, f32[4,128,768]{2,1,0:T(8,128)S(1)}, u32[]{:S(2)}, u32[]{:S(2)}) collective-permute-start(f32[4,128,768]{2,1,0:T(8,128)} %get-tuple-element.45), channel_id=1, source_target_pairs={{0,16},{16,32},{32,48},{48,64},{64,80},{80,96},{96,112},{1,17},{17... | collective-permute-start | bytes 4718600 | tf_op jit(solution)/shard_map/ppermute | solution.py:500
  143.8 69.8 %collective-permute-start.11 = (f32[4,128,768]{2,1,0:T(8,128)}, f32[4,128,768]{2,1,0:T(8,128)}, u32[]{:S(2)}, u32[]{:S(2)}) collective-permute-start(f32[4,128,768]{2,1,0:T(8,128)} %get-tuple-element.46), channel_id=1, source_target_pairs={{16,0},{32,16},{48,32},{64,48},{80,64},{96,80},{112,96},{17,1},{33... | collective-permute-start | bytes 4718600 | tf_op jit(solution)/shard_map/ppermute | solution.py:500
  202.3 21.0 %collective-permute-start.16 = (f32[3,128,512]{2,1,0:T(8,128)}, f32[3,128,512]{2,1,0:T(8,128)}, u32[]{:S(2)}, u32[]{:S(2)}) collective-permute-start(f32[3,128,512]{2,1,0:T(8,128)} %get-tuple-element.54), channel_id=1, source_target_pairs={{0,16},{16,32},{32,48},{48,64},{64,80},{80,96},{96,112},{1,17},{17... | collective-permute-start | bytes 2359304 | tf_op jit(solution)/shard_map/ppermute | solution.py:500
  204.3 1.3 copy-start.2
  209.3 44.5 %collective-permute-start.20 = (f32[5,128,512]{2,1,0:T(8,128)}, f32[5,128,512]{2,1,0:T(8,128)S(1)}, u32[]{:S(2)}, u32[]{:S(2)}) collective-permute-start(f32[5,128,512]{2,1,0:T(8,128)} %get-tuple-element.61), channel_id=1, source_target_pairs={{0,16},{16,32},{32,48},{48,64},{64,80},{80,96},{96,112},{1,17},{17... | collective-permute-start | bytes 3932168 | tf_op jit(solution)/shard_map/ppermute | solution.py:500
  211.2 42.6 %collective-permute-start.21 = (f32[5,128,512]{2,1,0:T(8,128)}, f32[5,128,512]{2,1,0:T(8,128)}, u32[]{:S(2)}, u32[]{:S(2)}) collective-permute-start(f32[5,128,512]{2,1,0:T(8,128)} %get-tuple-element.62), channel_id=1, source_target_pairs={{16,0},{32,16},{48,32},{64,48},{80,64},{96,80},{112,96},{17,1},{33... | collective-permute-start | bytes 3932168 | tf_op jit(solution)/shard_map/ppermute | solution.py:500
  213.6 1.2 copy-start.3
  218.0 52.2 %collective-permute-start.12 = (f32[4,512,128]{2,1,0:T(8,128)}, f32[4,512,128]{2,1,0:T(8,128)S(1)}, u32[]{:S(2)}, u32[]{:S(2)}) collective-permute-start(f32[4,512,128]{2,1,0:T(8,128)} %get-tuple-element.47), channel_id=1, source_target_pairs={{0,1},{1,2},{2,3},{3,4},{4,5},{5,6},{6,7},{7,8},{8,9},{9,10},{10,1... | collective-permute-start | bytes 3145736 | tf_op jit(solution)/shard_map/ppermute | solution.py:500
  220.1 50.2 %collective-permute-start.13 = (f32[4,512,128]{2,1,0:T(8,128)}, f32[4,512,128]{2,1,0:T(8,128)S(1)}, u32[]{:S(2)}, u32[]{:S(2)}) collective-permute-start(f32[4,512,128]{2,1,0:T(8,128)} %get-tuple-element.48), channel_id=1, source_target_pairs={{1,0},{2,1},{3,2},{4,3},{5,4},{6,5},{7,6},{8,7},{9,8},{10,9},{11,1... | collective-permute-start | bytes 3145736 | tf_op jit(solution)/shard_map/ppermute | solution.py:500
  223.4 15.7 %collective-permute-start.17 = (f32[3,128,512]{2,1,0:T(8,128)}, f32[3,128,512]{2,1,0:T(8,128)}, u32[]{:S(2)}, u32[]{:S(2)}) collective-permute-start(f32[3,128,512]{2,1,0:T(8,128)} %get-tuple-element.55), channel_id=1, source_target_pairs={{16,0},{32,16},{48,32},{64,48},{80,64},{96,80},{112,96},{17,1},{33... | collective-permute-start | bytes 2359304 | tf_op jit(solution)/shard_map/ppermute | solution.py:500
  253.8 1.1 copy-start.4
  270.2 1.0 copy-start.12
  270.2 1.3 copy-start.13
